TPU v7x, 32 devices: a whole 2x2x4 slice. The times are simulated.
32 devices in a mesh: fiber: 2 (over y), gx: 8 (over z, x), gy: 2 (over core).
Axes of the slice: x: 2, y: 2, z: 4, core: 2. Of those that a mesh axis runs over, the one named last changes fastest.
Arguments:
- optical_phase: bfloat16 [3072, 1024], P(('fiber', 'gx'), 'gy'), parts along dimension 0, may hold values from -6 to 6
- gauge_length: int32 [8], P('fiber'), parts along dimension 0, may hold values from 8 to 16, as said below
- snap_starts: int32 [32], P(('fiber', 'gx')), parts along dimension 0, may hold values from 0 to 64, as said below
- partner_offsets: int32 [8, 2], P('fiber'), parts along dimension 0, may hold values from -3 to 3, as said below
Outputs:
- gram_tiles: bfloat16 [4, 256, 4, 2, 256, 256], P('fiber', ('gx', 'gy')), parts along dimension 0
There are 2 independent parts, one for each index of `fiber`. A program takes and returns all parts, laid end to end along the dimension named above; each array names one. Nothing has to cross between parts.
Inputs may be any that keep to these rules, and one draw needn't show every extreme that they name: `gauge_length`: some block uses exactly 16. Snapshot s starts at sample (s // 2) * 192 + snap_starts[s] of the window and lies within that stretch of 192 samples; some snapshot has start 0 and some has 64. `partner_offsets`: block b's partners b + offset lie inside the fiber and differ from b; block 0 has the last block as a partner and the last block has block 0.
All inputs are finite; a program needn't handle non-finite values.
Results may differ from a plain program's by a relative error of at most 0.007.
Values may be sent and summed in bfloat16 or wider, within the bound.
No kernel may reach another device: no remote copies, remote signals or barrier semaphores. Data moves between devices by JAX's collectives and lax.ppermute only.
A program may use at most 128 MiB of HBM per device.

v0:
```python
import functools
import math

import jax
import jax.numpy as jnp
from jax import lax
from jax.experimental import pallas as pl
from jax.experimental.pallas import tpu as pltpu
from jax.sharding import PartitionSpec as P


BINS = 256
BLOCK = 256
SNAP_LEN = 128
GAUGE_MAX = 16
PARTNERS = 2
LANES = 128


def fourier_table(bin_index, total_len):
    sample = jnp.arange(SNAP_LEN, dtype=jnp.int32)
    product = bin_index[:, None] * sample[None, :] % total_len
    angles = 2.0 * math.pi / total_len * product.astype(jnp.float32)
    factor = 1.0 / math.sqrt(SNAP_LEN)
    return jnp.stack([jnp.cos(angles) * factor, -jnp.sin(angles) * factor]).astype(jnp.bfloat16)


def taper_window():
    sample = jnp.arange(SNAP_LEN, dtype=jnp.int32).astype(jnp.float32)
    return 0.5 - 0.5 * jnp.cos(2.0 * math.pi / SNAP_LEN * sample)


def ring_order(count):
    return [*range(0, count, 2), *range(count - 1, 0, -2)]


def starts_in(extra, snaps):
    values = extra.astype(jnp.float32).astype(jnp.int32)
    return [values[n * (8 // snaps), 0] for n in range(snaps)]


def shifted_table(base, starts):
    return jnp.concatenate([pltpu.roll(base, start, 1) for start in starts], axis=0).astype(jnp.bfloat16)


def spectra_kernel(snaps, base_ref, *refs):
    near_ref, far_ref, held_ref, sems = refs[-4:]
    stretches = refs[:-4]
    copies = [
        pltpu.make_async_copy(ref, held_ref.at[n], sems.at[n]) for n, ref in enumerate(stretches)
    ]
    for c in copies:
        c.start()
    rows = held_ref.shape[1] - 8
    tiles = near_ref.shape[0]
    each = base_ref.shape[0] // 2
    for n in range(len(stretches)):
        copies[n].wait()
        table = shifted_table(base_ref[...], starts_in(held_ref[n, rows:, :], snaps))[:, :rows]
        out = jnp.dot(table, held_ref[n, :rows, :], preferred_element_type=jnp.float32)
        for snap in range(snaps):
            for part, ref in enumerate((near_ref, far_ref)):
                at = (snap * 2 + part) * each
                to = (n * snaps + snap) * each
                for tile in range(tiles):
                    ref[tile, to : to + each, :] = out[at : at + each, tile * LANES : (tile + 1) * LANES]


def spectra_group(snaps, base, stretches):
    rows, half = stretches[0].shape
    each = base.shape[0] // 2
    count = len(stretches)
    shape = jax.ShapeDtypeStruct((half // LANES, count * snaps * each, LANES), jnp.float32)
    vmem = pl.BlockSpec(memory_space=pltpu.VMEM)
    return pl.pallas_call(
        functools.partial(spectra_kernel, snaps),
        in_specs=[vmem] + [pl.BlockSpec(memory_space=pl.ANY)] * count,
        out_specs=(vmem, vmem),
        out_shape=(shape, shape),
        scratch_shapes=[
            pltpu.VMEM((count, rows, half), jnp.bfloat16),
            pltpu.SemaphoreType.DMA((count,)),
        ],
        cost_estimate=pl.CostEstimate(
            flops=count * 100_000_000, bytes_accessed=count * 400_000, transcendentals=0
        ),
        compiler_params=pltpu.CompilerParams(vmem_limit_bytes=8 << 20),
        name="spectra",
    )(base, *stretches)


def gram_kernel(
    groups, snaps, scale, slots, unroll, meta_ref, base_ref, *refs
):
    early = refs[: 2 * groups]
    last = refs[2 * groups : 2 * groups + 4]
    out_ref, spectra_ref, last_ref, extra_ref, right_ref, buf_ref, early_sems, last_sems, sems = refs[2 * groups + 4 :]
    side = lax.axis_index("gy")
    bins = out_ref.shape[1]
    tiles, total, _ = spectra_ref.shape
    half = tiles // 2
    blocks = tiles * LANES // BLOCK
    each = 2 * bins
    cut = last[0].shape[0]
    rows = last_ref.shape[1]
    cores = (pl.ds(side * half, half), pl.ds((1 - side) * half, half))

    waits, done = [], 0
    for n, ref in enumerate(early):
        at = pl.ds(done, ref.shape[1])
        waits.append(pltpu.make_async_copy(ref, spectra_ref.at[cores[n % 2], at], early_sems.at[n]))
        done += ref.shape[1] * (n % 2)
    for n, ref in enumerate(last):
        at = pl.ds(0, cut) if n % 2 == 0 else pl.ds(cut, rows - cut)
        piece = ref if n % 2 == 0 else ref.at[pl.ds(0, rows - cut)]
        waits.append(pltpu.make_async_copy(piece, last_ref.at[n // 2, at], last_sems.at[n]))
    waits.append(pltpu.make_async_copy(last[1].at[pl.ds(rows - cut, 8)], extra_ref, last_sems.at[4]))
    for c in waits:
        c.start()
    waits[-1].wait()
    table = shifted_table(base_ref[:each, :], starts_in(extra_ref[...], snaps))[:, :rows]
    for c in waits[2 * groups : -1]:
        c.wait()
    for core in range(2):
        out = jnp.dot(table, last_ref[core], preferred_element_type=jnp.float32)
        for tile in range(half):
            place = side * half + tile if core == 0 else (1 - side) * half + tile
            spectra_ref[place, done:, :] = out[:, tile * LANES : (tile + 1) * LANES]
    for c in waits[: 2 * groups]:
        c.wait()

    def copies(f, slot):
        return [
            pltpu.make_async_copy(buf_ref.at[slot, part], out_ref.at[part, f], sems.at[slot, part])
            for part in range(2)
        ]

    def strain_spectra(row):
        held = [spectra_ref[tile, pl.ds(row, total // each, stride=each), :] for tile in range(tiles)]
        held.append(jnp.broadcast_to(held[-1][:, LANES - 1 :], held[-1].shape))
        per_block = BLOCK // LANES
        span = BLOCK + LANES
        for blk in range(blocks):
            wide = jnp.concatenate(held[blk * per_block : (blk + 1) * per_block + 1], axis=1)
            moved = pltpu.roll(wide, span - meta_ref[blk], 1)[:, :BLOCK]
            yield (moved - wide[:, :BLOCK]).astype(jnp.bfloat16)

    def one(f, slot, place):
        many = total // each
        for blk, (real, imag) in enumerate(zip(strain_spectra(f), strain_spectra(bins + f), strict=True)):
            right_ref[place, blk, :many, :BLOCK] = real
            right_ref[place, blk, many:, :BLOCK] = imag
            right_ref[place, blk, :many, BLOCK:] = imag
            right_ref[place, blk, many:, BLOCK:] = -real
        for blk in range(blocks):
            for k in range(PARTNERS):
                tile = lax.dot_general(
                    right_ref[place, blk, :, :BLOCK],
                    right_ref[place, blk + meta_ref[blocks * (1 + k) + blk]],
                    (((0,), (0,)), ((), ())),
                    preferred_element_type=jnp.float32,
                )
                if scale != 1.0:
                    tile = tile * scale
                buf_ref[slot, 0, blk, k] = tile[:, :BLOCK].astype(jnp.bfloat16)
                buf_ref[slot, 1, blk, k] = tile[:, BLOCK:].astype(jnp.bfloat16)
        for c in copies(f, slot):
            c.start()

    def step(i, carry):
        for u in range(unroll):
            f = i * unroll + u

            @pl.when(f >= slots)
            def _(f=f):
                for c in copies(f - slots, lax.rem(f, slots)):
                    c.wait()

        for u in range(unroll):
            f = i * unroll + u
            one(f, lax.rem(f, slots), u)
        return carry

    lax.fori_loop(0, bins // unroll, step, 0)
    for f in range(bins - slots, bins):
        for c in copies(f, f % slots):
            c.wait()


def gram(count, snaps, scale, meta, base, early, own, sib):
    half = early[0].shape[0]
    bins = base.shape[0] // 4
    blocks = 2 * half * LANES // BLOCK
    rows = sum(piece.shape[0] for piece in own) - 8
    total = count * snaps * 2 * bins
    slots, unroll = 4, 2
    vmem, smem = pl.BlockSpec(memory_space=pltpu.VMEM), pl.BlockSpec(memory_space=pltpu.SMEM)
    return pl.pallas_call(
        functools.partial(gram_kernel, len(early) // 2, snaps, scale, slots, unroll),
        in_specs=[smem, vmem] + [pl.BlockSpec(memory_space=pl.ANY)] * (len(early) + 4),
        out_specs=pl.BlockSpec(memory_space=pltpu.HBM),
        out_shape=jax.ShapeDtypeStruct((2, bins, blocks, PARTNERS, BLOCK, BLOCK), jnp.bfloat16),
        scratch_shapes=[
            pltpu.VMEM((2 * half, total, LANES), jnp.float32),
            pltpu.VMEM((2, rows, half * LANES), jnp.bfloat16),
            pltpu.VMEM((8, half * LANES), jnp.bfloat16),
            pltpu.VMEM((unroll, blocks, 2 * count * snaps, 2 * BLOCK), jnp.bfloat16),
            pltpu.VMEM((slots, 2, blocks, PARTNERS, BLOCK, BLOCK), jnp.bfloat16),
            pltpu.SemaphoreType.DMA((len(early),)),
            pltpu.SemaphoreType.DMA((5,)),
            pltpu.SemaphoreType.DMA((slots, 2)),
        ],
        compiler_params=pltpu.CompilerParams(vmem_limit_bytes=24 << 20),
        name="gram",
    )(meta, base, *early, *own, *sib)


def on_device_ring(optical_phase, gauge_length, snap_starts, partner_offsets):
    count = lax.axis_size("gx")
    pair_devices = lax.axis_size("gy")
    rows_local = optical_phase.shape[0]
    bins_dev = BINS // (count * pair_devices)
    snaps = snap_starts.shape[0]
    order = ring_order(count)
    ahead = [(order[i], order[(i + 1) % count]) for i in range(count)]
    back = [(b, a) for a, b in ahead]

    scale = 1.0 / math.sqrt(count * snaps)
    root = math.sqrt(scale)
    if math.frexp(root)[0] == 0.5:
        fold, scale = root, 1.0
    else:
        fold = 1.0

    cores = lax.axis_index("gy") ^ jnp.arange(pair_devices, dtype=jnp.int32)
    first_bin = (lax.axis_index("gx") * pair_devices + cores) * bins_dev
    bin_index = (first_bin[:, None] + jnp.arange(bins_dev, dtype=jnp.int32)[None, :]).reshape(-1)
    fourier = fourier_table(bin_index, 2 * BINS).astype(jnp.float32) * (taper_window() * fold)
    base = fourier.astype(jnp.bfloat16).astype(jnp.float32).reshape(2, pair_devices, bins_dev, SNAP_LEN)
    base = jnp.transpose(base, (1, 0, 2, 3)).reshape(2 * pair_devices * bins_dev, SNAP_LEN)
    base = jnp.pad(base, ((0, 0), (0, SNAP_LEN)))

    def exchange(x):
        return lax.ppermute(x, "gy", [(0, 1), (1, 0)])

    def tie(*xs):
        return lax.optimization_barrier(xs)

    def spectra(*stretches):
        return spectra_group(snaps, base, stretches)

    def onward(f, b):
        return lax.ppermute(f, "gx", ahead), lax.ppermute(b, "gx", back)

    half_rows = rows_local // 2
    half = optical_phase.shape[1]
    extra = snap_starts.astype(optical_phase.dtype)[:, None, None]
    extra = jnp.broadcast_to(extra, (snaps, 8 // snaps, half)).reshape(8, half)
    f1, b1 = onward(optical_phase, optical_phase)
    ef, eb = lax.ppermute(extra, "gx", ahead), lax.ppermute(extra, "gx", back)
    f1, b1 = jnp.concatenate([f1, ef]), jnp.concatenate([b1, eb])
    own = jnp.concatenate([optical_phase, extra])
    meta = jnp.concatenate([gauge_length, partner_offsets.T.reshape(-1)])
    f1, b1, own, base, meta = tie(f1, b1, own, base, meta)
    f2, b2 = onward(f1, b1)
    near1, far1 = spectra(own, f1, b1)
    f2, b2, near1, far1 = tie(f2, b2, near1, far1)
    f3, b3 = onward(f2, b2)
    other1 = exchange(far1)
    near2, far2 = spectra(f2, b2)
    f3, b3, near2, far2 = tie(f3, b3, near2, far2)
    f4, b4 = onward(f3[:half_rows], b3[half_rows:])
    other2 = exchange(far2)
    near3, far3 = spectra(f3, b3)
    f4, b4, near3, far3 = tie(f4, b4, near3, far3)
    own4, sib4 = (f4, b4), (exchange(f4), exchange(b4))
    other3 = exchange(far3)
    early = (near1, other1, near2, other2, near3, other3)
    return gram(count, snaps, scale, meta, base, early, own4, sib4)


def strain_blocks(extended, gauges):
    blocks = gauges.shape[0]
    block_first = jnp.arange(blocks, dtype=jnp.int32) * BLOCK

    def pick_block(column):
        return lax.dynamic_slice_in_dim(extended, column, BLOCK, 1)

    shifted = jax.vmap(pick_block)(block_first + gauges)
    initial = extended[:, : blocks * BLOCK].reshape(extended.shape[0], blocks, BLOCK)
    return shifted - jnp.transpose(initial, (1, 0, 2))


def tapered_segments(strain, start_rows):
    window = taper_window()

    def segment_at(row_start):
        return lax.dynamic_slice_in_dim(strain, row_start, SNAP_LEN, 1)

    segments = jax.vmap(segment_at)(start_rows)
    return (window[None, None, :, None] * segments).astype(jnp.bfloat16)


def spectra_for(tapered, bin_index):
    fourier = fourier_table(bin_index, 2 * BINS)
    spectrum = jnp.einsum("cft,sbtj->scfbj", fourier, tapered, preferred_element_type=jnp.float32)
    shape_out = spectrum.shape
    return spectrum.astype(jnp.bfloat16).reshape(
        shape_out[0], 2, shape_out[2], shape_out[3] * BLOCK
    )


def on_device(optical_phase, gauge_length, snap_starts, partner_offsets):
    time_devices = lax.axis_size("gx")
    pair_devices = lax.axis_size("gy")
    pair_index = lax.axis_index("gy")
    rows_local = optical_phase.shape[0]
    bins_dev = BINS // (time_devices * pair_devices)
    whole_phase = lax.all_gather(optical_phase, "gy", axis=1, tiled=True)
    edge_cols = jnp.broadcast_to(whole_phase[:, -1:], (rows_local, GAUGE_MAX))
    extended = jnp.concatenate([whole_phase, edge_cols], axis=1).astype(jnp.float32)
    strain = strain_blocks(extended, gauge_length)
    tapered = tapered_segments(strain, snap_starts)
    owner_slot = jnp.arange(time_devices * bins_dev, dtype=jnp.int32)
    bin_index = (
        owner_slot // bins_dev * pair_devices + pair_index
    ) * bins_dev + owner_slot % bins_dev
    spectra = spectra_for(tapered, bin_index)
    gathered = lax.all_to_all(spectra, "gx", split_axis=2, concat_axis=0, tiled=True)
    snaps_all = gathered.shape[0]
    blocks_all = gathered.shape[3] // BLOCK
    spectra_blocks = gathered.reshape(snaps_all, 2, bins_dev, blocks_all, BLOCK)
    partners = jnp.arange(blocks_all, dtype=jnp.int32)[:, None] + partner_offsets
    partner_data = jnp.take(spectra_blocks, partners.reshape(-1), axis=3)
    partner_data = partner_data.reshape(snaps_all, 2, bins_dev, blocks_all, PARTNERS, BLOCK)
    swapped = jnp.stack([partner_data[:, 1], -partner_data[:, 0]], axis=1)
    stacked = jnp.stack([partner_data, swapped])
    gram_tile = jnp.einsum(
        "scfbi,pscfbkj->pfbkij", spectra_blocks, stacked, preferred_element_type=jnp.float32
    )
    return (gram_tile * (1.0 / math.sqrt(snaps_all))).astype(jnp.bfloat16)


def solution(mesh):
    in_specs = (P(("fiber", "gx"), "gy"), P("fiber"), P(("fiber", "gx")), P("fiber", None))
    out_specs = P("fiber", ("gx", "gy"), None, None, None, None)

    def body(optical_phase, gauge_length, snap_starts, partner_offsets):
        ring = lax.axis_size("gx") == 8 and lax.axis_size("gy") == 2 and snap_starts.shape[0] == 2
        plan = on_device_ring if ring else on_device
        return plan(optical_phase, gauge_length, snap_starts, partner_offsets)

    return jax.shard_map(body, mesh=mesh, in_specs=in_specs, out_specs=out_specs, check_vma=False)
```

profile of v0, /device:TPU:0, one launch (start us, length us, event | category | flops | bytes accessed | tf_op | source)
XLA Modules:
  0.0 49.5 jit_solution(17796840529048929665)
XLA Ops:
  0.0 0.7 %convert_element_type.40 = bf16[2]{0:T(256)(128)(2,1)S(1)} convert(s32[2]{0:T(128)} %param.6) | non-fusion elementwise | flops 2 | bytes 12 | tf_op jit(solution)/shard_map/convert_element_type | solution.py:257
  0.7 0.1 broadcast_in_dim.6
  0.7 0.1 broadcast_in_dim.7
  0.8 0.1 broadcast_in_dim.16
  0.9 3.0 %collective-permute-start.3 = (bf16[8,512]{1,0:T(8,128)(2,1)S(1)}, bf16[8,512]{1,0:T(8,128)(2,1)S(1)}, u32[]{:S(2)}, u32[]{:S(2)}) collective-permute-start(bf16[8,512]{1,0:T(8,128)(2,1)S(1)} %broadcast_in_dim.16), channel_id=1, source_target_pairs={{4,0},{8,4},{12,8},{14,12},{10,14},{6,10},{2,6},{0,2},{5,1},{9,5},... | collective-permute-start | bytes 24584 | tf_op jit(solution)/shard_map/ppermute | solution.py:260
  3.9 0.1 collective-permute-start.1
  4.0 2.0 %collective-permute-start = (bf16[192,512]{1,0:T(8,128)(2,1)}, bf16[192,512]{1,0:T(8,128)(2,1)S(1)}, u32[]{:S(2)}, u32[]{:S(2)}) collective-permute-start(bf16[192,512]{1,0:T(8,128)(2,1)} %param.4), channel_id=1, source_target_pairs={{0,4},{4,8},{8,12},{12,14},{14,10},{10,6},{6,2},{2,0},{1,5},{5,9},... | collective-permute-start | bytes 589832 | tf_op jit(solution)/shard_map/ppermute | solution.py:253
  6.0 0.0 collective-permute-start.2
  6.0 1.0 %pad_maximum_fusion.2.refs_0_ = bf16[200,512]{1,0:T(8,128)(2,1)S(1)} fusion(bf16[8,512]{1,0:T(8,128)(2,1)S(1)} %broadcast_in_dim.16, bf16[192,512]{1,0:T(8,128)(2,1)} %param.4), kind=kLoop, calls=%fused_computation.2 | loop fusion | flops 409600 | bytes 409600 | tf_op jit(solution)/shard_map/concatenate | solution.py:262
  7.0 0.8 %reshape.140 = s32[8]{0:T(128)S(1)} reshape(s32[2,4]{1,0:T(2,128)} %bitcast.5) | data formatting | bytes 64 | tf_op jit(solution)/shard_map/reshape | solution.py:263
  7.8 0.1 iota_add_fusion
  7.8 0.2 multiply_convert_fusion.2
  8.0 0.7 %pad_add_fusion.meta_ref = s32[12]{0:T(128)S(1)} fusion(s32[8]{0:T(128)S(1)} %reshape.140, s32[4]{0:T(128)} %param.5), kind=kLoop, calls=%fused_computation.17 | loop fusion | flops 12 | bytes 96 | tf_op jit(solution)/shard_map/concatenate | solution.py:263
  8.8 0.0 collective-permute-done.1
  8.8 1.9 %collective-permute-done = bf16[192,512]{1,0:T(8,128)(2,1)S(1)} collective-permute-done((bf16[192,512]{1,0:T(8,128)(2,1)}, bf16[192,512]{1,0:T(8,128)(2,1)S(1)}, u32[]{:S(2)}, u32[]{:S(2)}) %collective-permute-start) | collective-permute-done | bytes 196640 | tf_op jit(solution)/shard_map/ppermute | solution.py:253
  10.6 0.0 collective-permute-done.3
  10.6 1.3 %collective-permute-done.2 = bf16[192,512]{1,0:T(8,128)(2,1)S(1)} collective-permute-done((bf16[192,512]{1,0:T(8,128)(2,1)}, bf16[192,512]{1,0:T(8,128)(2,1)S(1)}, u32[]{:S(2)}, u32[]{:S(2)}) %collective-permute-start.2) | collective-permute-done | bytes 196640 | tf_op jit(solution)/shard_map/ppermute | solution.py:253
  12.0 1.6 %collective-permute-start.4 = (bf16[200,512]{1,0:T(8,128)(2,1)S(1)}, bf16[200,512]{1,0:T(8,128)(2,1)S(1)}, u32[]{:S(2)}, u32[]{:S(2)}) collective-permute-start(bf16[200,512]{1,0:T(8,128)(2,1)S(1)} %pad_maximum_fusion.refs_1_), channel_id=1, source_target_pairs={{0,4},{4,8},{8,12},{12,14},{14,10},{10,6},{6,2},{2,0},{1,5},{5,9},... | collective-permute-start | bytes 614408 | tf_op jit(solution)/shard_map/ppermute | solution.py:253
  13.6 0.4 collective-permute-start.5
  14.1 1.6 %spectra.3 = (f32[4,192,128]{2,1,0:T(8,128)S(1)}, f32[4,192,128]{2,1,0:T(8,128)S(1)}) custom-call(f32[64,256]{1,0:T(8,128)S(1)} %pad_convert_fusion.base_ref, bf16[200,512]{1,0:T(8,128)(2,1)S(1)} %pad_maximum_fusion.2.refs_0_, bf16[200,512]{1,0:T(8,128)(2,1)S(1)} %pad_maximum_fusion.refs_1_, bf16[200,512]{1,0:T(8,128)(2,1)S(1)} %pad_maximum_fusion.1.refs_2_), custom_call_target="tpu_custom_call" | custom-call | flops 300000000 | bytes 1200000 | tf_op jit(solution)/shard_map/spectra/pallas_call | solution.py:75
  15.7 2.1 %collective-permute-done.4.refs_0_ = bf16[200,512]{1,0:T(8,128)(2,1)S(1)} collective-permute-done((bf16[200,512]{1,0:T(8,128)(2,1)S(1)}, bf16[200,512]{1,0:T(8,128)(2,1)S(1)}, u32[]{:S(2)}, u32[]{:S(2)}) %collective-permute-start.4) | collective-permute-done | bytes 204832 | tf_op jit(solution)/shard_map/ppermute | solution.py:253
  17.8 1.6 %collective-permute-done.5.refs_1_ = bf16[200,512]{1,0:T(8,128)(2,1)S(1)} collective-permute-done((bf16[200,512]{1,0:T(8,128)(2,1)S(1)}, bf16[200,512]{1,0:T(8,128)(2,1)S(1)}, u32[]{:S(2)}, u32[]{:S(2)}) %collective-permute-start.5) | collective-permute-done | bytes 204832 | tf_op jit(solution)/shard_map/ppermute | solution.py:253
  19.4 1.6 %collective-permute-start.7 = (bf16[200,512]{1,0:T(8,128)(2,1)S(1)}, bf16[200,512]{1,0:T(8,128)(2,1)S(1)}, u32[]{:S(2)}, u32[]{:S(2)}) collective-permute-start(bf16[200,512]{1,0:T(8,128)(2,1)S(1)} %collective-permute-done.4.refs_0_), channel_id=1, source_target_pairs={{0,4},{4,8},{8,12},{12,14},{14,10},{10,6},{6,2},{2,0},{1,5},{5,9},... | collective-permute-start | bytes 614408 | tf_op jit(solution)/shard_map/ppermute | solution.py:253
  21.0 0.4 collective-permute-start.8
  21.4 0.0 collective-permute-start.6
  21.4 1.1 %spectra.4 = (f32[4,128,128]{2,1,0:T(8,128)S(1)}, f32[4,128,128]{2,1,0:T(8,128)S(1)}) custom-call(f32[64,256]{1,0:T(8,128)S(1)} %pad_convert_fusion.base_ref, bf16[200,512]{1,0:T(8,128)(2,1)S(1)} %collective-permute-done.4.refs_0_, bf16[200,512]{1,0:T(8,128)(2,1)S(1)} %collective-permute-done.5.refs_1_), custom_call_target="tpu_custom_call" | custom-call | flops 200000000 | bytes 800000 | tf_op jit(solution)/shard_map/spectra/pallas_call | solution.py:75
  22.5 2.7 %collective-permute-done.7.refs_0_ = bf16[200,512]{1,0:T(8,128)(2,1)S(1)} collective-permute-done((bf16[200,512]{1,0:T(8,128)(2,1)S(1)}, bf16[200,512]{1,0:T(8,128)(2,1)S(1)}, u32[]{:S(2)}, u32[]{:S(2)}) %collective-permute-start.7) | collective-permute-done | bytes 204832 | tf_op jit(solution)/shard_map/ppermute | solution.py:253
  25.2 2.6 %collective-permute-done.8.refs_1_ = bf16[200,512]{1,0:T(8,128)(2,1)S(1)} collective-permute-done((bf16[200,512]{1,0:T(8,128)(2,1)S(1)}, bf16[200,512]{1,0:T(8,128)(2,1)S(1)}, u32[]{:S(2)}, u32[]{:S(2)}) %collective-permute-start.8) | collective-permute-done | bytes 204832 | tf_op jit(solution)/shard_map/ppermute | solution.py:253
  27.8 0.5 %collective-permute-start.11 = (bf16[104,512]{1,0:T(8,128)(2,1)S(1)}, bf16[104,512]{1,0:T(8,128)(2,1)S(1)}, u32[]{:S(2)}, u32[]{:S(2)}) collective-permute-start(bf16[104,512]{1,0:T(8,128)(2,1)S(1)} %slice.7), channel_id=1, source_target_pairs={{4,0},{8,4},{12,8},{14,12},{10,14},{6,10},{2,6},{0,2},{5,1},{9,5},... | collective-permute-start | bytes 319496 | tf_op jit(solution)/shard_map/ppermute | solution.py:253
  28.3 1.6 %collective-permute-start.10 = (bf16[96,512]{1,0:T(8,128)(2,1)S(1)}, bf16[96,512]{1,0:T(8,128)(2,1)S(1)}, u32[]{:S(2)}, u32[]{:S(2)}) collective-permute-start(bf16[96,512]{1,0:T(8,128)(2,1)S(1)} %slice.6), channel_id=1, source_target_pairs={{0,4},{4,8},{8,12},{12,14},{14,10},{10,6},{6,2},{2,0},{1,5},{5,9},... | collective-permute-start | bytes 294920 | tf_op jit(solution)/shard_map/ppermute | solution.py:253
  29.9 0.0 collective-permute-start.9
  29.9 1.1 %spectra.5 = (f32[4,128,128]{2,1,0:T(8,128)S(1)}, f32[4,128,128]{2,1,0:T(8,128)S(1)}) custom-call(f32[64,256]{1,0:T(8,128)S(1)} %pad_convert_fusion.base_ref, bf16[200,512]{1,0:T(8,128)(2,1)S(1)} %collective-permute-done.7.refs_0_, bf16[200,512]{1,0:T(8,128)(2,1)S(1)} %collective-permute-done.8.refs_1_), custom_call_target="tpu_custom_call" | custom-call | flops 200000000 | bytes 800000 | tf_op jit(solution)/shard_map/spectra/pallas_call | solution.py:75
  31.0 2.0 %collective-permute-done.10.refs_6_ = bf16[96,512]{1,0:T(8,128)(2,1)S(1)} collective-permute-done((bf16[96,512]{1,0:T(8,128)(2,1)S(1)}, bf16[96,512]{1,0:T(8,128)(2,1)S(1)}, u32[]{:S(2)}, u32[]{:S(2)}) %collective-permute-start.10) | collective-permute-done | bytes 98336 | tf_op jit(solution)/shard_map/ppermute | solution.py:253
  33.0 0.0 collective-permute-done.11.refs_7_
  33.0 0.0 collective-permute-start.12
  33.0 0.5 %collective-permute-start.14 = (bf16[104,512]{1,0:T(8,128)(2,1)S(1)}, bf16[104,512]{1,0:T(8,128)(2,1)S(1)}, u32[]{:S(2)}, u32[]{:S(2)}) collective-permute-start(bf16[104,512]{1,0:T(8,128)(2,1)S(1)} %collective-permute-done.11.refs_7_), channel_id=1, source_target_pairs={{0,1},{1,0},{2,3},{3,2},{4,5},{5,4},{6,7},{7,6},{8,9},{9,8},{10,11... | collective-permute-start | bytes 319496 | tf_op jit(solution)/shard_map/ppermute | solution.py:244
  33.5 0.0 collective-permute-start.13
  33.5 0.0 collective-permute-done.6.refs_1_
  33.5 1.3 %collective-permute-done.13.refs_8_ = bf16[96,512]{1,0:T(8,128)(2,1)S(1)} collective-permute-done((bf16[96,512]{1,0:T(8,128)(2,1)S(1)}, bf16[96,512]{1,0:T(8,128)(2,1)S(1)}, u32[]{:S(2)}, u32[]{:S(2)}) %collective-permute-start.13) | collective-permute-done | bytes 98336 | tf_op jit(solution)/shard_map/ppermute | solution.py:244
  34.8 0.0 collective-permute-done.14.refs_9_
  34.8 0.0 collective-permute-done.9.refs_3_
  34.8 0.0 collective-permute-done.12.refs_5_
  34.8 14.7 %gram.1 = bf16[2,16,4,2,256,256]{5,4,3,2,1,0:T(8,128)(2,1)} custom-call(s32[12]{0:T(128)S(1)} %pad_add_fusion.meta_ref, f32[64,256]{1,0:T(8,128)S(1)} %pad_convert_fusion.base_ref, f32[4,192,128]{2,1,0:T(8,128)S(1)} %get-tuple-element.35.refs_0_, f32[4,192,128]{2,1,0:T(8,128)S(1)} %collective-permute-done.6.refs_1_, ...), custom_call_target="tpu_custom_call" | custom-call | tf_op jit(solution)/shard_map/gram/pallas_call | solution.py:198
  (8 shorter events, 0.1 us)
Async XLA Ops:
  0.9 9.7 %collective-permute-start.3 = (bf16[8,512]{1,0:T(8,128)(2,1)S(1)}, bf16[8,512]{1,0:T(8,128)(2,1)S(1)}, u32[]{:S(2)}, u32[]{:S(2)}) collective-permute-start(bf16[8,512]{1,0:T(8,128)(2,1)S(1)} %broadcast_in_dim.16), channel_id=1, source_target_pairs={{4,0},{8,4},{12,8},{14,12},{10,14},{6,10},{2,6},{0,2},{5,1},{9,5},... | collective-permute-start | bytes 24584 | tf_op jit(solution)/shard_map/ppermute | solution.py:260
  3.9 4.9 %collective-permute-start.1 = (bf16[8,512]{1,0:T(8,128)(2,1)S(1)}, bf16[8,512]{1,0:T(8,128)(2,1)S(1)}, u32[]{:S(2)}, u32[]{:S(2)}) collective-permute-start(bf16[8,512]{1,0:T(8,128)(2,1)S(1)} %broadcast_in_dim.16), channel_id=1, source_target_pairs={{0,4},{4,8},{8,12},{12,14},{14,10},{10,6},{6,2},{2,0},{1,5},{5,9},... | collective-permute-start | bytes 24584 | tf_op jit(solution)/shard_map/ppermute | solution.py:260
  4.0 6.7 %collective-permute-start = (bf16[192,512]{1,0:T(8,128)(2,1)}, bf16[192,512]{1,0:T(8,128)(2,1)S(1)}, u32[]{:S(2)}, u32[]{:S(2)}) collective-permute-start(bf16[192,512]{1,0:T(8,128)(2,1)} %param.4), channel_id=1, source_target_pairs={{0,4},{4,8},{8,12},{12,14},{14,10},{10,6},{6,2},{2,0},{1,5},{5,9},... | collective-permute-start | bytes 589832 | tf_op jit(solution)/shard_map/ppermute | solution.py:253
  6.0 6.0 %collective-permute-start.2 = (bf16[192,512]{1,0:T(8,128)(2,1)}, bf16[192,512]{1,0:T(8,128)(2,1)S(1)}, u32[]{:S(2)}, u32[]{:S(2)}) collective-permute-start(bf16[192,512]{1,0:T(8,128)(2,1)} %param.4), channel_id=1, source_target_pairs={{4,0},{8,4},{12,8},{14,12},{10,14},{6,10},{2,6},{0,2},{5,1},{9,5},... | collective-permute-start | bytes 589832 | tf_op jit(solution)/shard_map/ppermute | solution.py:253
  12.0 5.8 %collective-permute-start.4 = (bf16[200,512]{1,0:T(8,128)(2,1)S(1)}, bf16[200,512]{1,0:T(8,128)(2,1)S(1)}, u32[]{:S(2)}, u32[]{:S(2)}) collective-permute-start(bf16[200,512]{1,0:T(8,128)(2,1)S(1)} %pad_maximum_fusion.refs_1_), channel_id=1, source_target_pairs={{0,4},{4,8},{8,12},{12,14},{14,10},{10,6},{6,2},{2,0},{1,5},{5,9},... | collective-permute-start | bytes 614408 | tf_op jit(solution)/shard_map/ppermute | solution.py:253
  13.6 5.8 %collective-permute-start.5 = (bf16[200,512]{1,0:T(8,128)(2,1)S(1)}, bf16[200,512]{1,0:T(8,128)(2,1)S(1)}, u32[]{:S(2)}, u32[]{:S(2)}) collective-permute-start(bf16[200,512]{1,0:T(8,128)(2,1)S(1)} %pad_maximum_fusion.1.refs_2_), channel_id=1, source_target_pairs={{4,0},{8,4},{12,8},{14,12},{10,14},{6,10},{2,6},{0,2},{5,1},{9,5},... | collective-permute-start | bytes 614408 | tf_op jit(solution)/shard_map/ppermute | solution.py:253
  19.4 5.8 %collective-permute-start.7 = (bf16[200,512]{1,0:T(8,128)(2,1)S(1)}, bf16[200,512]{1,0:T(8,128)(2,1)S(1)}, u32[]{:S(2)}, u32[]{:S(2)}) collective-permute-start(bf16[200,512]{1,0:T(8,128)(2,1)S(1)} %collective-permute-done.4.refs_0_), channel_id=1, source_target_pairs={{0,4},{4,8},{8,12},{12,14},{14,10},{10,6},{6,2},{2,0},{1,5},{5,9},... | collective-permute-start | bytes 614408 | tf_op jit(solution)/shard_map/ppermute | solution.py:253
  21.0 6.8 %collective-permute-start.8 = (bf16[200,512]{1,0:T(8,128)(2,1)S(1)}, bf16[200,512]{1,0:T(8,128)(2,1)S(1)}, u32[]{:S(2)}, u32[]{:S(2)}) collective-permute-start(bf16[200,512]{1,0:T(8,128)(2,1)S(1)} %collective-permute-done.5.refs_1_), channel_id=1, source_target_pairs={{4,0},{8,4},{12,8},{14,12},{10,14},{6,10},{2,6},{0,2},{5,1},{9,5},... | collective-permute-start | bytes 614408 | tf_op jit(solution)/shard_map/ppermute | solution.py:253
  21.4 12.1 %collective-permute-start.6 = (f32[4,192,128]{2,1,0:T(8,128)S(1)}, f32[4,192,128]{2,1,0:T(8,128)S(1)}, u32[]{:S(2)}, u32[]{:S(2)}) collective-permute-start(f32[4,192,128]{2,1,0:T(8,128)S(1)} %get-tuple-element.36), channel_id=1, source_target_pairs={{0,1},{1,0},{2,3},{3,2},{4,5},{5,4},{6,7},{7,6},{8,9},{9,8},{10,11... | collective-permute-start | bytes 1179656 | tf_op jit(solution)/shard_map/ppermute | solution.py:244
  27.8 5.2 %collective-permute-start.11 = (bf16[104,512]{1,0:T(8,128)(2,1)S(1)}, bf16[104,512]{1,0:T(8,128)(2,1)S(1)}, u32[]{:S(2)}, u32[]{:S(2)}) collective-permute-start(bf16[104,512]{1,0:T(8,128)(2,1)S(1)} %slice.7), channel_id=1, source_target_pairs={{4,0},{8,4},{12,8},{14,12},{10,14},{6,10},{2,6},{0,2},{5,1},{9,5},... | collective-permute-start | bytes 319496 | tf_op jit(solution)/shard_map/ppermute | solution.py:253
  28.3 4.7 %collective-permute-start.10 = (bf16[96,512]{1,0:T(8,128)(2,1)S(1)}, bf16[96,512]{1,0:T(8,128)(2,1)S(1)}, u32[]{:S(2)}, u32[]{:S(2)}) collective-permute-start(bf16[96,512]{1,0:T(8,128)(2,1)S(1)} %slice.6), channel_id=1, source_target_pairs={{0,4},{4,8},{8,12},{12,14},{14,10},{10,6},{6,2},{2,0},{1,5},{5,9},... | collective-permute-start | bytes 294920 | tf_op jit(solution)/shard_map/ppermute | solution.py:253
  29.9 4.9 %collective-permute-start.9 = (f32[4,128,128]{2,1,0:T(8,128)S(1)}, f32[4,128,128]{2,1,0:T(8,128)S(1)}, u32[]{:S(2)}, u32[]{:S(2)}) collective-permute-start(f32[4,128,128]{2,1,0:T(8,128)S(1)} %get-tuple-element.42), channel_id=1, source_target_pairs={{0,1},{1,0},{2,3},{3,2},{4,5},{5,4},{6,7},{7,6},{8,9},{9,8},{10,11... | collective-permute-start | bytes 786440 | tf_op jit(solution)/shard_map/ppermute | solution.py:244
  33.0 1.8 %collective-permute-start.12 = (f32[4,128,128]{2,1,0:T(8,128)S(1)}, f32[4,128,128]{2,1,0:T(8,128)S(1)}, u32[]{:S(2)}, u32[]{:S(2)}) collective-permute-start(f32[4,128,128]{2,1,0:T(8,128)S(1)} %get-tuple-element.48), channel_id=1, source_target_pairs={{0,1},{1,0},{2,3},{3,2},{4,5},{5,4},{6,7},{7,6},{8,9},{9,8},{10,11... | collective-permute-start | bytes 786440 | tf_op jit(solution)/shard_map/ppermute | solution.py:244
  33.0 1.8 %collective-permute-start.14 = (bf16[104,512]{1,0:T(8,128)(2,1)S(1)}, bf16[104,512]{1,0:T(8,128)(2,1)S(1)}, u32[]{:S(2)}, u32[]{:S(2)}) collective-permute-start(bf16[104,512]{1,0:T(8,128)(2,1)S(1)} %collective-permute-done.11.refs_7_), channel_id=1, source_target_pairs={{0,1},{1,0},{2,3},{3,2},{4,5},{5,4},{6,7},{7,6},{8,9},{9,8},{10,11... | collective-permute-start | bytes 319496 | tf_op jit(solution)/shard_map/ppermute | solution.py:244
  33.5 1.3 %collective-permute-start.13 = (bf16[96,512]{1,0:T(8,128)(2,1)S(1)}, bf16[96,512]{1,0:T(8,128)(2,1)S(1)}, u32[]{:S(2)}, u32[]{:S(2)}) collective-permute-start(bf16[96,512]{1,0:T(8,128)(2,1)S(1)} %collective-permute-done.10.refs_6_), channel_id=1, source_target_pairs={{0,1},{1,0},{2,3},{3,2},{4,5},{5,4},{6,7},{7,6},{8,9},{9,8},{10,11... | collective-permute-start | bytes 294920 | tf_op jit(solution)/shard_map/ppermute | solution.py:244
where the time goes:
time: 49.7 us; the launch traced here: 49.5 us
  Pallas kernels  18.4 us (37%)
  waiting for transfers between devices  15.5 us (31%)
  starting transfers between devices  11.8 us (24%)
  other arithmetic  2.68 us (5%)
  local copies, waits for them, and re-layouts  1.01 us (2%)
    pallas_call x1, Pallas kernels, gram(): pl.pallas_call(functools.partial(gram_kernel, len(early) // 2, snaps, sca...  14.7 us
    ppermute x8, waiting for transfers between devices, onward(): return (lax.ppermute(f, 'gx', ahead), lax.ppermute(b, 'gx', back))  14.2 us
    ppermute x8, starting transfers between devices, onward(): return (lax.ppermute(f, 'gx', ahead), lax.ppermute(b, 'gx', back))  8.25 us
    pallas_call x3, Pallas kernels, spectra_group(): pl.pallas_call(functools.partial(spectra_kernel, snaps), in_specs=[vmem]...  3.71 us
    ppermute x2, starting transfers between devices, on_device_ring(): ef, eb = (lax.ppermute(extra, 'gx', ahead), lax.ppermute(extra, 'gx', back))  3.05 us
    ppermute x5, waiting for transfers between devices, exchange(): return lax.ppermute(x, 'gy', [(0, 1), (1, 0)])  1.32 us
  transfers between devices with their start and end apart: 15, of which 8 were waited for; matrix products, arithmetic and copies ran while one was open for 6% of the time, Pallas kernels for 7%

commit v1 on v0

--- a/solution.py
+++ b/solution.py
@@ -44,43 +44,32 @@
 
 
 def spectra_kernel(snaps, base_ref, *refs):
-    near_ref, far_ref, held_ref, sems = refs[-4:]
-    stretches = refs[:-4]
-    copies = [
-        pltpu.make_async_copy(ref, held_ref.at[n], sems.at[n]) for n, ref in enumerate(stretches)
-    ]
-    for c in copies:
-        c.start()
-    rows = held_ref.shape[1] - 8
+    *stretches, near_ref, far_ref = refs
+    rows = stretches[0].shape[0] - 8
     tiles = near_ref.shape[0]
     each = base_ref.shape[0] // 2
-    for n in range(len(stretches)):
-        copies[n].wait()
-        table = shifted_table(base_ref[...], starts_in(held_ref[n, rows:, :], snaps))[:, :rows]
-        out = jnp.dot(table, held_ref[n, :rows, :], preferred_element_type=jnp.float32)
+    for n, ref in enumerate(stretches):
+        table = shifted_table(base_ref[...], starts_in(ref[rows:, :], snaps))[:, :rows]
+        out = jnp.dot(table, ref[:rows, :], preferred_element_type=jnp.float32)
         for snap in range(snaps):
-            for part, ref in enumerate((near_ref, far_ref)):
+            for part, to_ref in enumerate((near_ref, far_ref)):
                 at = (snap * 2 + part) * each
                 to = (n * snaps + snap) * each
                 for tile in range(tiles):
-                    ref[tile, to : to + each, :] = out[at : at + each, tile * LANES : (tile + 1) * LANES]
+                    to_ref[tile, to : to + each, :] = out[at : at + each, tile * LANES : (tile + 1) * LANES]
 
 
 def spectra_group(snaps, base, stretches):
-    rows, half = stretches[0].shape
+    half = stretches[0].shape[1]
     each = base.shape[0] // 2
     count = len(stretches)
     shape = jax.ShapeDtypeStruct((half // LANES, count * snaps * each, LANES), jnp.float32)
     vmem = pl.BlockSpec(memory_space=pltpu.VMEM)
     return pl.pallas_call(
         functools.partial(spectra_kernel, snaps),
-        in_specs=[vmem] + [pl.BlockSpec(memory_space=pl.ANY)] * count,
+        in_specs=[vmem] * (1 + count),
         out_specs=(vmem, vmem),
         out_shape=(shape, shape),
-        scratch_shapes=[
-            pltpu.VMEM((count, rows, half), jnp.bfloat16),
-            pltpu.SemaphoreType.DMA((count,)),
-        ],
         cost_estimate=pl.CostEstimate(
             flops=count * 100_000_000, bytes_accessed=count * 400_000, transcendentals=0
         ),
@@ -89,45 +78,33 @@
     )(base, *stretches)
 
 
-def gram_kernel(
-    groups, snaps, scale, slots, unroll, meta_ref, base_ref, *refs
-):
+def gram_kernel(groups, snaps, scale, slots, meta_ref, base_ref, *refs):
     early = refs[: 2 * groups]
-    last = refs[2 * groups : 2 * groups + 4]
-    out_ref, spectra_ref, last_ref, extra_ref, right_ref, buf_ref, early_sems, last_sems, sems = refs[2 * groups + 4 :]
+    own0, own1, sib0, sib1 = refs[2 * groups : 2 * groups + 4]
+    out_ref, spectra_ref, even_ref, odd_ref, buf_ref, sems = refs[2 * groups + 4 :]
     side = lax.axis_index("gy")
     bins = out_ref.shape[1]
     tiles, total, _ = spectra_ref.shape
     half = tiles // 2
     blocks = tiles * LANES // BLOCK
     each = 2 * bins
-    cut = last[0].shape[0]
-    rows = last_ref.shape[1]
-    cores = (pl.ds(side * half, half), pl.ds((1 - side) * half, half))
-
-    waits, done = [], 0
+    many = total // each
+    rows = own0.shape[0] + own1.shape[0] - 8
+    cut = own0.shape[0]
+
+    done = 0
     for n, ref in enumerate(early):
-        at = pl.ds(done, ref.shape[1])
-        waits.append(pltpu.make_async_copy(ref, spectra_ref.at[cores[n % 2], at], early_sems.at[n]))
+        side_of = side if n % 2 == 0 else 1 - side
+        for tile in range(half):
+            spectra_ref[side_of * half + tile, done : done + ref.shape[1], :] = ref[tile]
         done += ref.shape[1] * (n % 2)
-    for n, ref in enumerate(last):
-        at = pl.ds(0, cut) if n % 2 == 0 else pl.ds(cut, rows - cut)
-        piece = ref if n % 2 == 0 else ref.at[pl.ds(0, rows - cut)]
-        waits.append(pltpu.make_async_copy(piece, last_ref.at[n // 2, at], last_sems.at[n]))
-    waits.append(pltpu.make_async_copy(last[1].at[pl.ds(rows - cut, 8)], extra_ref, last_sems.at[4]))
-    for c in waits:
-        c.start()
-    waits[-1].wait()
-    table = shifted_table(base_ref[:each, :], starts_in(extra_ref[...], snaps))[:, :rows]
-    for c in waits[2 * groups : -1]:
-        c.wait()
-    for core in range(2):
-        out = jnp.dot(table, last_ref[core], preferred_element_type=jnp.float32)
+    table = shifted_table(base_ref[:each, :], starts_in(own1[rows - cut :, :], snaps))[:, :rows]
+    for core, (lower, upper) in enumerate(((own0, own1), (sib0, sib1))):
+        phase = jnp.concatenate([lower[...], upper[: rows - cut, :]], axis=0)
+        out = jnp.dot(table, phase, preferred_element_type=jnp.float32)
+        side_of = side if core == 0 else 1 - side
         for tile in range(half):
-            place = side * half + tile if core == 0 else (1 - side) * half + tile
-            spectra_ref[place, done:, :] = out[:, tile * LANES : (tile + 1) * LANES]
-    for c in waits[: 2 * groups]:
-        c.wait()
+            spectra_ref[side_of * half + tile, done:, :] = out[:, tile * LANES : (tile + 1) * LANES]
 
     def copies(f, slot):
         return [
@@ -136,7 +113,7 @@
         ]
 
     def strain_spectra(row):
-        held = [spectra_ref[tile, pl.ds(row, total // each, stride=each), :] for tile in range(tiles)]
+        held = [spectra_ref[tile, pl.ds(row, many, stride=each), :] for tile in range(tiles)]
         held.append(jnp.broadcast_to(held[-1][:, LANES - 1 :], held[-1].shape))
         per_block = BLOCK // LANES
         span = BLOCK + LANES
@@ -145,18 +122,27 @@
             moved = pltpu.roll(wide, span - meta_ref[blk], 1)[:, :BLOCK]
             yield (moved - wide[:, :BLOCK]).astype(jnp.bfloat16)
 
-    def one(f, slot, place):
-        many = total // each
+    def prepare(f, to_ref):
         for blk, (real, imag) in enumerate(zip(strain_spectra(f), strain_spectra(bins + f), strict=True)):
-            right_ref[place, blk, :many, :BLOCK] = real
-            right_ref[place, blk, many:, :BLOCK] = imag
-            right_ref[place, blk, :many, BLOCK:] = imag
-            right_ref[place, blk, many:, BLOCK:] = -real
+            to_ref[blk, :many, :BLOCK] = real
+            to_ref[blk, many:, :BLOCK] = imag
+            to_ref[blk, :many, BLOCK:] = imag
+            to_ref[blk, many:, BLOCK:] = -real
+
+    def multiply(f, from_ref):
+        slot = lax.rem(f, slots)
+
+        @pl.when(f >= slots)
+        def _():
+            for c in copies(f - slots, slot):
+                c.wait()
+
         for blk in range(blocks):
+            left = from_ref[blk, :, :BLOCK]
             for k in range(PARTNERS):
                 tile = lax.dot_general(
-                    right_ref[place, blk, :, :BLOCK],
-                    right_ref[place, blk + meta_ref[blocks * (1 + k) + blk]],
+                    left,
+                    from_ref[blk + meta_ref[blocks * (1 + k) + blk]],
                     (((0,), (0,)), ((), ())),
                     preferred_element_type=jnp.float32,
                 )
@@ -168,20 +154,14 @@
             c.start()
 
     def step(i, carry):
-        for u in range(unroll):
-            f = i * unroll + u
-
-            @pl.when(f >= slots)
-            def _(f=f):
-                for c in copies(f - slots, lax.rem(f, slots)):
-                    c.wait()
-
-        for u in range(unroll):
-            f = i * unroll + u
-            one(f, lax.rem(f, slots), u)
+        prepare(2 * i + 1, odd_ref)
+        multiply(2 * i, even_ref)
+        prepare(lax.rem(2 * i + 2, bins), even_ref)
+        multiply(2 * i + 1, odd_ref)
         return carry
 
-    lax.fori_loop(0, bins // unroll, step, 0)
+    prepare(0, even_ref)
+    lax.fori_loop(0, bins // 2, step, 0)
     for f in range(bins - slots, bins):
         for c in copies(f, f % slots):
             c.wait()
@@ -191,23 +171,19 @@
     half = early[0].shape[0]
     bins = base.shape[0] // 4
     blocks = 2 * half * LANES // BLOCK
-    rows = sum(piece.shape[0] for piece in own) - 8
     total = count * snaps * 2 * bins
-    slots, unroll = 4, 2
+    slots = 4
     vmem, smem = pl.BlockSpec(memory_space=pltpu.VMEM), pl.BlockSpec(memory_space=pltpu.SMEM)
     return pl.pallas_call(
-        functools.partial(gram_kernel, len(early) // 2, snaps, scale, slots, unroll),
-        in_specs=[smem, vmem] + [pl.BlockSpec(memory_space=pl.ANY)] * (len(early) + 4),
+        functools.partial(gram_kernel, len(early) // 2, snaps, scale, slots),
+        in_specs=[smem] + [vmem] * (1 + len(early) + 4),
         out_specs=pl.BlockSpec(memory_space=pltpu.HBM),
         out_shape=jax.ShapeDtypeStruct((2, bins, blocks, PARTNERS, BLOCK, BLOCK), jnp.bfloat16),
         scratch_shapes=[
             pltpu.VMEM((2 * half, total, LANES), jnp.float32),
-            pltpu.VMEM((2, rows, half * LANES), jnp.bfloat16),
-            pltpu.VMEM((8, half * LANES), jnp.bfloat16),
-            pltpu.VMEM((unroll, blocks, 2 * count * snaps, 2 * BLOCK), jnp.bfloat16),
+            pltpu.VMEM((blocks, 2 * count * snaps, 2 * BLOCK), jnp.bfloat16),
+            pltpu.VMEM((blocks, 2 * count * snaps, 2 * BLOCK), jnp.bfloat16),
             pltpu.VMEM((slots, 2, blocks, PARTNERS, BLOCK, BLOCK), jnp.bfloat16),
-            pltpu.SemaphoreType.DMA((len(early),)),
-            pltpu.SemaphoreType.DMA((5,)),
             pltpu.SemaphoreType.DMA((slots, 2)),
         ],
         compiler_params=pltpu.CompilerParams(vmem_limit_bytes=24 << 20),
@@ -261,18 +237,15 @@
     f1, b1 = jnp.concatenate([f1, ef]), jnp.concatenate([b1, eb])
     own = jnp.concatenate([optical_phase, extra])
     meta = jnp.concatenate([gauge_length, partner_offsets.T.reshape(-1)])
-    f1, b1, own, base, meta = tie(f1, b1, own, base, meta)
+    f1, own, base, meta = tie(f1, own, base, meta)
     f2, b2 = onward(f1, b1)
     near1, far1 = spectra(own, f1, b1)
-    f2, b2, near1, far1 = tie(f2, b2, near1, far1)
     f3, b3 = onward(f2, b2)
     other1 = exchange(far1)
     near2, far2 = spectra(f2, b2)
-    f3, b3, near2, far2 = tie(f3, b3, near2, far2)
     f4, b4 = onward(f3[:half_rows], b3[half_rows:])
     other2 = exchange(far2)
     near3, far3 = spectra(f3, b3)
-    f4, b4, near3, far3 = tie(f4, b4, near3, far3)
     own4, sib4 = (f4, b4), (exchange(f4), exchange(b4))
     other3 = exchange(far3)
     early = (near1, other1, near2, other2, near3, other3)

time: 49.7 us -> 48.6 us (0.978)
  Pallas kernels: 18.4 us -> 17 us
  starting transfers between devices: 11.8 us -> 12.4 us
    pallas_call x3, Pallas kernels: 3.71 us -> 0.96 us  [spectra_group(): pl.pallas_call(functools.partial(spectra_kernel, snaps), in_specs=[vmem]...]
    pallas_call x1, Pallas kernels: 14.7 us -> 16.1 us  [gram(): pl.pallas_call(functools.partial(gram_kernel, len(early) // 2, snaps, sca...]
  transfers between devices with their start and end apart: 15 -> 15, of which waited for: 8 -> 9; matrix products, arithmetic and copies ran while one was open for 6% -> 6% of each run, Pallas kernels for 7% -> 2%
where the time goes in v1:
time: 48.6 us; the launch traced here: 48.4 us
  Pallas kernels  17 us (35%)
  waiting for transfers between devices  15.2 us (31%)
  starting transfers between devices  12.4 us (26%)
  other arithmetic  2.66 us (5%)
  local copies, waits for them, and re-layouts  1.03 us (2%)
    pallas_call x1, Pallas kernels, gram(): pl.pallas_call(functools.partial(gram_kernel, len(early) // 2, snaps, sca...  16.1 us
    ppermute x8, waiting for transfers between devices, onward(): return (lax.ppermute(f, 'gx', ahead), lax.ppermute(b, 'gx', back))  13.9 us
    ppermute x8, starting transfers between devices, onward(): return (lax.ppermute(f, 'gx', ahead), lax.ppermute(b, 'gx', back))  8.64 us
    ppermute x2, starting transfers between devices, on_device_ring(): ef, eb = (lax.ppermute(extra, 'gx', ahead), lax.ppermute(extra, 'gx', back))  3.05 us
    ppermute x5, waiting for transfers between devices, exchange(): return lax.ppermute(x, 'gy', [(0, 1), (1, 0)])  1.3 us
  transfers between devices with their start and end apart: 15, of which 9 were waited for; matrix products, arithmetic and copies ran while one was open for 6% of the time, Pallas kernels for 2%

profile of v1, /device:TPU:0, one launch (start us, length us, event | category | flops | bytes accessed | tf_op | source)
XLA Modules:
  0.0 48.4 jit_solution(14264591607564502263)
XLA Ops:
  0.0 0.7 %convert_element_type.40 = bf16[2]{0:T(256)(128)(2,1)S(1)} convert(s32[2]{0:T(128)} %param.6) | non-fusion elementwise | flops 2 | bytes 12 | tf_op jit(solution)/shard_map/convert_element_type | solution.py:233
  0.7 0.1 broadcast_in_dim.6
  0.7 0.1 broadcast_in_dim.7
  0.8 0.1 broadcast_in_dim.16
  0.9 3.0 %collective-permute-start.3 = (bf16[8,512]{1,0:T(8,128)(2,1)S(1)}, bf16[8,512]{1,0:T(8,128)(2,1)S(1)}, u32[]{:S(2)}, u32[]{:S(2)}) collective-permute-start(bf16[8,512]{1,0:T(8,128)(2,1)S(1)} %broadcast_in_dim.16), channel_id=1, source_target_pairs={{4,0},{8,4},{12,8},{14,12},{10,14},{6,10},{2,6},{0,2},{5,1},{9,5},... | collective-permute-start | bytes 24584 | tf_op jit(solution)/shard_map/ppermute | solution.py:236
  3.9 0.1 collective-permute-start.1
  4.0 2.0 %collective-permute-start = (bf16[192,512]{1,0:T(8,128)(2,1)}, bf16[192,512]{1,0:T(8,128)(2,1)S(1)}, u32[]{:S(2)}, u32[]{:S(2)}) collective-permute-start(bf16[192,512]{1,0:T(8,128)(2,1)} %param.4), channel_id=1, source_target_pairs={{0,4},{4,8},{8,12},{12,14},{14,10},{10,6},{6,2},{2,0},{1,5},{5,9},... | collective-permute-start | bytes 589832 | tf_op jit(solution)/shard_map/ppermute | solution.py:229
  6.0 0.0 collective-permute-start.2
  6.0 1.0 %pad_maximum_fusion.1.refs_0_ = bf16[200,512]{1,0:T(8,128)(2,1)S(1)} fusion(bf16[8,512]{1,0:T(8,128)(2,1)S(1)} %broadcast_in_dim.16, bf16[192,512]{1,0:T(8,128)(2,1)} %param.4), kind=kLoop, calls=%fused_computation.1 | loop fusion | flops 409600 | bytes 409600 | tf_op jit(solution)/shard_map/concatenate | solution.py:238
  7.0 0.8 %reshape.140 = s32[8]{0:T(128)S(1)} reshape(s32[2,4]{1,0:T(2,128)} %bitcast.5) | data formatting | bytes 64 | tf_op jit(solution)/shard_map/reshape | solution.py:239
  7.8 0.1 iota_add_fusion
  7.8 0.2 multiply_convert_fusion.2
  8.0 0.7 %pad_add_fusion.meta_ref = s32[12]{0:T(128)S(1)} fusion(s32[8]{0:T(128)S(1)} %reshape.140, s32[4]{0:T(128)} %param.5), kind=kLoop, calls=%fused_computation.18 | loop fusion | flops 12 | bytes 96 | tf_op jit(solution)/shard_map/concatenate | solution.py:239
  8.8 0.0 collective-permute-done.1
  8.8 1.9 %collective-permute-done = bf16[192,512]{1,0:T(8,128)(2,1)S(1)} collective-permute-done((bf16[192,512]{1,0:T(8,128)(2,1)}, bf16[192,512]{1,0:T(8,128)(2,1)S(1)}, u32[]{:S(2)}, u32[]{:S(2)}) %collective-permute-start) | collective-permute-done | bytes 196640 | tf_op jit(solution)/shard_map/ppermute | solution.py:229
  10.6 1.4 %collective-permute-done.2 = bf16[192,512]{1,0:T(8,128)(2,1)S(1)} collective-permute-done((bf16[192,512]{1,0:T(8,128)(2,1)}, bf16[192,512]{1,0:T(8,128)(2,1)S(1)}, u32[]{:S(2)}, u32[]{:S(2)}) %collective-permute-start.2) | collective-permute-done | bytes 196640 | tf_op jit(solution)/shard_map/ppermute | solution.py:229
  12.0 0.0 collective-permute-done.3
  12.0 0.4 collective-permute-start.6
  12.4 1.7 %collective-permute-start.5 = (bf16[200,512]{1,0:T(8,128)(2,1)S(1)}, bf16[200,512]{1,0:T(8,128)(2,1)S(1)}, u32[]{:S(2)}, u32[]{:S(2)}) collective-permute-start(bf16[200,512]{1,0:T(8,128)(2,1)S(1)} %pad_maximum_fusion.refs_1_), channel_id=1, source_target_pairs={{0,4},{4,8},{8,12},{12,14},{14,10},{10,6},{6,2},{2,0},{1,5},{5,9},... | collective-permute-start | bytes 614408 | tf_op jit(solution)/shard_map/ppermute | solution.py:229
  14.1 4.1 %collective-permute-done.6.refs_1_ = bf16[200,512]{1,0:T(8,128)(2,1)S(1)} collective-permute-done((bf16[200,512]{1,0:T(8,128)(2,1)S(1)}, bf16[200,512]{1,0:T(8,128)(2,1)S(1)}, u32[]{:S(2)}, u32[]{:S(2)}) %collective-permute-start.6) | collective-permute-done | bytes 204832 | tf_op jit(solution)/shard_map/ppermute | solution.py:229
  18.3 0.0 collective-permute-start.9
  18.3 0.1 collective-permute-done.5.refs_0_
  18.4 2.2 %collective-permute-start.8 = (bf16[200,512]{1,0:T(8,128)(2,1)S(1)}, bf16[200,512]{1,0:T(8,128)(2,1)S(1)}, u32[]{:S(2)}, u32[]{:S(2)}) collective-permute-start(bf16[200,512]{1,0:T(8,128)(2,1)S(1)} %collective-permute-done.5.refs_0_), channel_id=1, source_target_pairs={{0,4},{4,8},{8,12},{12,14},{14,10},{10,6},{6,2},{2,0},{1,5},{5,9},... | collective-permute-start | bytes 614408 | tf_op jit(solution)/shard_map/ppermute | solution.py:229
  20.6 0.3 spectra.3
  20.9 0.1 collective-permute-start.4
  21.0 0.3 spectra.4
  21.3 0.6 %collective-permute-start.7 = (f32[4,128,128]{2,1,0:T(8,128)S(1)}, f32[4,128,128]{2,1,0:T(8,128)S(1)}, u32[]{:S(2)}, u32[]{:S(2)}) collective-permute-start(f32[4,128,128]{2,1,0:T(8,128)S(1)} %get-tuple-element.22), channel_id=1, source_target_pairs={{0,1},{1,0},{2,3},{3,2},{4,5},{5,4},{6,7},{7,6},{8,9},{9,8},{10,11... | collective-permute-start | bytes 786440 | tf_op jit(solution)/shard_map/ppermute | solution.py:220
  21.9 2.1 %collective-permute-done.9.refs_1_ = bf16[200,512]{1,0:T(8,128)(2,1)S(1)} collective-permute-done((bf16[200,512]{1,0:T(8,128)(2,1)S(1)}, bf16[200,512]{1,0:T(8,128)(2,1)S(1)}, u32[]{:S(2)}, u32[]{:S(2)}) %collective-permute-start.9) | collective-permute-done | bytes 204832 | tf_op jit(solution)/shard_map/ppermute | solution.py:229
  24.0 0.1 collective-permute-done.8.refs_0_
  24.1 0.3 spectra.5
  24.4 0.1 collective-permute-start.10
  24.5 1.6 %collective-permute-start.12 = (bf16[104,512]{1,0:T(8,128)(2,1)S(1)}, bf16[104,512]{1,0:T(8,128)(2,1)S(1)}, u32[]{:S(2)}, u32[]{:S(2)}) collective-permute-start(bf16[104,512]{1,0:T(8,128)(2,1)S(1)} %slice.9), channel_id=1, source_target_pairs={{4,0},{8,4},{12,8},{14,12},{10,14},{6,10},{2,6},{0,2},{5,1},{9,5},... | collective-permute-start | bytes 319496 | tf_op jit(solution)/shard_map/ppermute | solution.py:229
  26.1 0.8 %collective-permute-start.11 = (bf16[96,512]{1,0:T(8,128)(2,1)S(1)}, bf16[96,512]{1,0:T(8,128)(2,1)S(1)}, u32[]{:S(2)}, u32[]{:S(2)}) collective-permute-start(bf16[96,512]{1,0:T(8,128)(2,1)S(1)} %slice.8), channel_id=1, source_target_pairs={{0,4},{4,8},{8,12},{12,14},{14,10},{10,6},{6,2},{2,0},{1,5},{5,9},... | collective-permute-start | bytes 294920 | tf_op jit(solution)/shard_map/ppermute | solution.py:229
  26.9 3.5 %collective-permute-done.12.refs_7_ = bf16[104,512]{1,0:T(8,128)(2,1)S(1)} collective-permute-done((bf16[104,512]{1,0:T(8,128)(2,1)S(1)}, bf16[104,512]{1,0:T(8,128)(2,1)S(1)}, u32[]{:S(2)}, u32[]{:S(2)}) %collective-permute-start.12) | collective-permute-done | bytes 106528 | tf_op jit(solution)/shard_map/ppermute | solution.py:229
  30.4 0.0 collective-permute-start.14
  30.4 0.7 %collective-permute-done.11.refs_6_ = bf16[96,512]{1,0:T(8,128)(2,1)S(1)} collective-permute-done((bf16[96,512]{1,0:T(8,128)(2,1)S(1)}, bf16[96,512]{1,0:T(8,128)(2,1)S(1)}, u32[]{:S(2)}, u32[]{:S(2)}) %collective-permute-start.11) | collective-permute-done | bytes 98336 | tf_op jit(solution)/shard_map/ppermute | solution.py:229
  31.1 0.0 collective-permute-start.13
  31.1 0.0 collective-permute-done.4.refs_1_
  31.1 0.0 collective-permute-done.7.refs_3_
  31.1 1.3 %collective-permute-done.13.refs_8_ = bf16[96,512]{1,0:T(8,128)(2,1)S(1)} collective-permute-done((bf16[96,512]{1,0:T(8,128)(2,1)S(1)}, bf16[96,512]{1,0:T(8,128)(2,1)S(1)}, u32[]{:S(2)}, u32[]{:S(2)}) %collective-permute-start.13) | collective-permute-done | bytes 98336 | tf_op jit(solution)/shard_map/ppermute | solution.py:220
  32.4 0.0 collective-permute-done.14.refs_9_
  32.4 0.0 collective-permute-done.10.refs_5_
  32.4 16.1 %gram.1 = bf16[2,16,4,2,256,256]{5,4,3,2,1,0:T(8,128)(2,1)} custom-call(s32[12]{0:T(128)S(1)} %pad_add_fusion.meta_ref, f32[64,256]{1,0:T(8,128)S(1)} %pad_convert_fusion.base_ref, f32[4,192,128]{2,1,0:T(8,128)S(1)} %get-tuple-element.19.refs_0_, f32[4,192,128]{2,1,0:T(8,128)S(1)} %collective-permute-done.4.refs_1_, ...), custom_call_target="tpu_custom_call" | custom-call | tf_op jit(solution)/shard_map/gram/pallas_call | solution.py:177
  (9 shorter events, 0.1 us)
Async XLA Ops:
  0.9 11.1 %collective-permute-start.3 = (bf16[8,512]{1,0:T(8,128)(2,1)S(1)}, bf16[8,512]{1,0:T(8,128)(2,1)S(1)}, u32[]{:S(2)}, u32[]{:S(2)}) collective-permute-start(bf16[8,512]{1,0:T(8,128)(2,1)S(1)} %broadcast_in_dim.16), channel_id=1, source_target_pairs={{4,0},{8,4},{12,8},{14,12},{10,14},{6,10},{2,6},{0,2},{5,1},{9,5},... | collective-permute-start | bytes 24584 | tf_op jit(solution)/shard_map/ppermute | solution.py:236
  3.9 4.9 %collective-permute-start.1 = (bf16[8,512]{1,0:T(8,128)(2,1)S(1)}, bf16[8,512]{1,0:T(8,128)(2,1)S(1)}, u32[]{:S(2)}, u32[]{:S(2)}) collective-permute-start(bf16[8,512]{1,0:T(8,128)(2,1)S(1)} %broadcast_in_dim.16), channel_id=1, source_target_pairs={{0,4},{4,8},{8,12},{12,14},{14,10},{10,6},{6,2},{2,0},{1,5},{5,9},... | collective-permute-start | bytes 24584 | tf_op jit(solution)/shard_map/ppermute | solution.py:236
  4.0 6.7 %collective-permute-start = (bf16[192,512]{1,0:T(8,128)(2,1)}, bf16[192,512]{1,0:T(8,128)(2,1)S(1)}, u32[]{:S(2)}, u32[]{:S(2)}) collective-permute-start(bf16[192,512]{1,0:T(8,128)(2,1)} %param.4), channel_id=1, source_target_pairs={{0,4},{4,8},{8,12},{12,14},{14,10},{10,6},{6,2},{2,0},{1,5},{5,9},... | collective-permute-start | bytes 589832 | tf_op jit(solution)/shard_map/ppermute | solution.py:229
  6.0 6.0 %collective-permute-start.2 = (bf16[192,512]{1,0:T(8,128)(2,1)}, bf16[192,512]{1,0:T(8,128)(2,1)S(1)}, u32[]{:S(2)}, u32[]{:S(2)}) collective-permute-start(bf16[192,512]{1,0:T(8,128)(2,1)} %param.4), channel_id=1, source_target_pairs={{4,0},{8,4},{12,8},{14,12},{10,14},{6,10},{2,6},{0,2},{5,1},{9,5},... | collective-permute-start | bytes 589832 | tf_op jit(solution)/shard_map/ppermute | solution.py:229
  12.0 6.2 %collective-permute-start.6 = (bf16[200,512]{1,0:T(8,128)(2,1)S(1)}, bf16[200,512]{1,0:T(8,128)(2,1)S(1)}, u32[]{:S(2)}, u32[]{:S(2)}) collective-permute-start(bf16[200,512]{1,0:T(8,128)(2,1)S(1)} %constant_dynamic-update-slice_fusion.refs_2_), channel_id=1, source_target_pairs={{4,0},{8,4},{12,8},{14,12},{10,14},{6,10},{2,6},{0,2},{5,1},{9,5},... | collective-permute-start | bytes 614408 | tf_op jit(solution)/shard_map/ppermute | solution.py:229
  12.4 6.0 %collective-permute-start.5 = (bf16[200,512]{1,0:T(8,128)(2,1)S(1)}, bf16[200,512]{1,0:T(8,128)(2,1)S(1)}, u32[]{:S(2)}, u32[]{:S(2)}) collective-permute-start(bf16[200,512]{1,0:T(8,128)(2,1)S(1)} %pad_maximum_fusion.refs_1_), channel_id=1, source_target_pairs={{0,4},{4,8},{8,12},{12,14},{14,10},{10,6},{6,2},{2,0},{1,5},{5,9},... | collective-permute-start | bytes 614408 | tf_op jit(solution)/shard_map/ppermute | solution.py:229
  18.3 5.8 %collective-permute-start.9 = (bf16[200,512]{1,0:T(8,128)(2,1)S(1)}, bf16[200,512]{1,0:T(8,128)(2,1)S(1)}, u32[]{:S(2)}, u32[]{:S(2)}) collective-permute-start(bf16[200,512]{1,0:T(8,128)(2,1)S(1)} %collective-permute-done.6.refs_1_), channel_id=1, source_target_pairs={{4,0},{8,4},{12,8},{14,12},{10,14},{6,10},{2,6},{0,2},{5,1},{9,5},... | collective-permute-start | bytes 614408 | tf_op jit(solution)/shard_map/ppermute | solution.py:229
  18.4 5.8 %collective-permute-start.8 = (bf16[200,512]{1,0:T(8,128)(2,1)S(1)}, bf16[200,512]{1,0:T(8,128)(2,1)S(1)}, u32[]{:S(2)}, u32[]{:S(2)}) collective-permute-start(bf16[200,512]{1,0:T(8,128)(2,1)S(1)} %collective-permute-done.5.refs_0_), channel_id=1, source_target_pairs={{0,4},{4,8},{8,12},{12,14},{14,10},{10,6},{6,2},{2,0},{1,5},{5,9},... | collective-permute-start | bytes 614408 | tf_op jit(solution)/shard_map/ppermute | solution.py:229
  20.9 10.2 %collective-permute-start.4 = (f32[4,192,128]{2,1,0:T(8,128)S(1)}, f32[4,192,128]{2,1,0:T(8,128)S(1)}, u32[]{:S(2)}, u32[]{:S(2)}) collective-permute-start(f32[4,192,128]{2,1,0:T(8,128)S(1)} %get-tuple-element.20), channel_id=1, source_target_pairs={{0,1},{1,0},{2,3},{3,2},{4,5},{5,4},{6,7},{7,6},{8,9},{9,8},{10,11... | collective-permute-start | bytes 1179656 | tf_op jit(solution)/shard_map/ppermute | solution.py:220
  21.3 9.8 %collective-permute-start.7 = (f32[4,128,128]{2,1,0:T(8,128)S(1)}, f32[4,128,128]{2,1,0:T(8,128)S(1)}, u32[]{:S(2)}, u32[]{:S(2)}) collective-permute-start(f32[4,128,128]{2,1,0:T(8,128)S(1)} %get-tuple-element.22), channel_id=1, source_target_pairs={{0,1},{1,0},{2,3},{3,2},{4,5},{5,4},{6,7},{7,6},{8,9},{9,8},{10,11... | collective-permute-start | bytes 786440 | tf_op jit(solution)/shard_map/ppermute | solution.py:220
  24.4 7.9 %collective-permute-start.10 = (f32[4,128,128]{2,1,0:T(8,128)S(1)}, f32[4,128,128]{2,1,0:T(8,128)S(1)}, u32[]{:S(2)}, u32[]{:S(2)}) collective-permute-start(f32[4,128,128]{2,1,0:T(8,128)S(1)} %get-tuple-element.24), channel_id=1, source_target_pairs={{0,1},{1,0},{2,3},{3,2},{4,5},{5,4},{6,7},{7,6},{8,9},{9,8},{10,11... | collective-permute-start | bytes 786440 | tf_op jit(solution)/shard_map/ppermute | solution.py:220
  24.5 5.9 %collective-permute-start.12 = (bf16[104,512]{1,0:T(8,128)(2,1)S(1)}, bf16[104,512]{1,0:T(8,128)(2,1)S(1)}, u32[]{:S(2)}, u32[]{:S(2)}) collective-permute-start(bf16[104,512]{1,0:T(8,128)(2,1)S(1)} %slice.9), channel_id=1, source_target_pairs={{4,0},{8,4},{12,8},{14,12},{10,14},{6,10},{2,6},{0,2},{5,1},{9,5},... | collective-permute-start | bytes 319496 | tf_op jit(solution)/shard_map/ppermute | solution.py:229
  26.1 5.0 %collective-permute-start.11 = (bf16[96,512]{1,0:T(8,128)(2,1)S(1)}, bf16[96,512]{1,0:T(8,128)(2,1)S(1)}, u32[]{:S(2)}, u32[]{:S(2)}) collective-permute-start(bf16[96,512]{1,0:T(8,128)(2,1)S(1)} %slice.8), channel_id=1, source_target_pairs={{0,4},{4,8},{8,12},{12,14},{14,10},{10,6},{6,2},{2,0},{1,5},{5,9},... | collective-permute-start | bytes 294920 | tf_op jit(solution)/shard_map/ppermute | solution.py:229
  30.4 2.0 %collective-permute-start.14 = (bf16[104,512]{1,0:T(8,128)(2,1)S(1)}, bf16[104,512]{1,0:T(8,128)(2,1)S(1)}, u32[]{:S(2)}, u32[]{:S(2)}) collective-permute-start(bf16[104,512]{1,0:T(8,128)(2,1)S(1)} %collective-permute-done.12.refs_7_), channel_id=1, source_target_pairs={{0,1},{1,0},{2,3},{3,2},{4,5},{5,4},{6,7},{7,6},{8,9},{9,8},{10,11... | collective-permute-start | bytes 319496 | tf_op jit(solution)/shard_map/ppermute | solution.py:220
  31.1 1.3 %collective-permute-start.13 = (bf16[96,512]{1,0:T(8,128)(2,1)S(1)}, bf16[96,512]{1,0:T(8,128)(2,1)S(1)}, u32[]{:S(2)}, u32[]{:S(2)}) collective-permute-start(bf16[96,512]{1,0:T(8,128)(2,1)S(1)} %collective-permute-done.11.refs_6_), channel_id=1, source_target_pairs={{0,1},{1,0},{2,3},{3,2},{4,5},{5,4},{6,7},{7,6},{8,9},{9,8},{10,11... | collective-permute-start | bytes 294920 | tf_op jit(solution)/shard_map/ppermute | solution.py:220

commit v2 on v1

--- a/solution.py
+++ b/solution.py
@@ -81,7 +81,7 @@
 def gram_kernel(groups, snaps, scale, slots, meta_ref, base_ref, *refs):
     early = refs[: 2 * groups]
     own0, own1, sib0, sib1 = refs[2 * groups : 2 * groups + 4]
-    out_ref, spectra_ref, even_ref, odd_ref, buf_ref, sems = refs[2 * groups + 4 :]
+    out_ref, spectra_ref, *operands, buf_ref, sems = refs[2 * groups + 4 :]
     side = lax.axis_index("gy")
     bins = out_ref.shape[1]
     tiles, total, _ = spectra_ref.shape
@@ -131,18 +131,12 @@
 
     def multiply(f, from_ref):
         slot = lax.rem(f, slots)
-
-        @pl.when(f >= slots)
-        def _():
-            for c in copies(f - slots, slot):
-                c.wait()
-
         for blk in range(blocks):
             left = from_ref[blk, :, :BLOCK]
             for k in range(PARTNERS):
                 tile = lax.dot_general(
                     left,
-                    from_ref[blk + meta_ref[blocks * (1 + k) + blk]],
+                    from_ref[meta_ref[blocks * (1 + k) + blk]],
                     (((0,), (0,)), ((), ())),
                     preferred_element_type=jnp.float32,
                 )
@@ -153,15 +147,26 @@
         for c in copies(f, slot):
             c.start()
 
+    def free(f):
+        @pl.when(f >= slots)
+        def _():
+            for n in (f, f + 1):
+                for c in copies(n - slots, lax.rem(n, slots)):
+                    c.wait()
+
     def step(i, carry):
-        prepare(2 * i + 1, odd_ref)
-        multiply(2 * i, even_ref)
-        prepare(lax.rem(2 * i + 2, bins), even_ref)
-        multiply(2 * i + 1, odd_ref)
+        f = 4 * i
+        for n in (0, 2):
+            free(f + n)
+            multiply(f + n, operands[n])
+            prepare(lax.rem(f + n + 2, bins), operands[2 - n])
+            multiply(f + n + 1, operands[n + 1])
+            prepare(lax.rem(f + n + 3, bins), operands[3 - n])
         return carry
 
-    prepare(0, even_ref)
-    lax.fori_loop(0, bins // 2, step, 0)
+    prepare(0, operands[0])
+    prepare(1, operands[1])
+    lax.fori_loop(0, bins // 4, step, 0)
     for f in range(bins - slots, bins):
         for c in copies(f, f % slots):
             c.wait()
@@ -181,8 +186,7 @@
         out_shape=jax.ShapeDtypeStruct((2, bins, blocks, PARTNERS, BLOCK, BLOCK), jnp.bfloat16),
         scratch_shapes=[
             pltpu.VMEM((2 * half, total, LANES), jnp.float32),
-            pltpu.VMEM((blocks, 2 * count * snaps, 2 * BLOCK), jnp.bfloat16),
-            pltpu.VMEM((blocks, 2 * count * snaps, 2 * BLOCK), jnp.bfloat16),
+            *[pltpu.VMEM((blocks, 2 * count * snaps, 2 * BLOCK), jnp.bfloat16)] * 4,
             pltpu.VMEM((slots, 2, blocks, PARTNERS, BLOCK, BLOCK), jnp.bfloat16),
             pltpu.SemaphoreType.DMA((slots, 2)),
         ],
@@ -226,7 +230,9 @@
         return spectra_group(snaps, base, stretches)
 
     def onward(f, b):
-        return lax.ppermute(f, "gx", ahead), lax.ppermute(b, "gx", back)
+        f = lax.ppermute(f, "gx", ahead)
+        b = lax.ppermute(b, "gx", back)
+        return f, b
 
     half_rows = rows_local // 2
     half = optical_phase.shape[1]
@@ -236,20 +242,22 @@
     ef, eb = lax.ppermute(extra, "gx", ahead), lax.ppermute(extra, "gx", back)
     f1, b1 = jnp.concatenate([f1, ef]), jnp.concatenate([b1, eb])
     own = jnp.concatenate([optical_phase, extra])
-    meta = jnp.concatenate([gauge_length, partner_offsets.T.reshape(-1)])
-    f1, own, base, meta = tie(f1, own, base, meta)
     f2, b2 = onward(f1, b1)
     near1, far1 = spectra(own, f1, b1)
+    f2, gauges, offsets = tie(f2, gauge_length, partner_offsets)
+    partners = offsets.T + jnp.arange(offsets.shape[0], dtype=jnp.int32)[None, :]
+    meta = jnp.concatenate([gauges, partners.reshape(-1)])
     f3, b3 = onward(f2, b2)
     other1 = exchange(far1)
     near2, far2 = spectra(f2, b2)
     f4, b4 = onward(f3[:half_rows], b3[half_rows:])
     other2 = exchange(far2)
     near3, far3 = spectra(f3, b3)
-    own4, sib4 = (f4, b4), (exchange(f4), exchange(b4))
+    s_b4 = exchange(b4)
+    s_f4 = exchange(f4)
     other3 = exchange(far3)
     early = (near1, other1, near2, other2, near3, other3)
-    return gram(count, snaps, scale, meta, base, early, own4, sib4)
+    return gram(count, snaps, scale, meta, base, early, (f4, b4), (s_f4, s_b4))
 
 
 def strain_blocks(extended, gauges):

time: 48.6 us -> 46.7 us (0.961)
  Pallas kernels: 17 us -> 14.3 us
  waiting for transfers between devices: 15.2 us -> 15.9 us
  local copies, waits for them, and re-layouts: 1.03 us -> 0.37 us
  other arithmetic: 2.66 us -> 3.31 us
    pallas_call x1, Pallas kernels: 16.1 us -> 13.3 us  [gram(): pl.pallas_call(functools.partial(gram_kernel, len(early) // 2, snaps, sca...]
    ppermute x8, waiting for transfers between devices: 13.9 us -> 15.6 us  [the longest x4 9.7 us: onward(): b = lax.ppermute(b, 'gx', back)]
    ppermute x5, waiting for transfers between devices: 1.3 us -> 0.23 us  [exchange(): return lax.ppermute(x, 'gy', [(0, 1), (1, 0)])]
    add x0 -> x1, other arithmetic: none -> 0.69 us  [on_device_ring(): offsets.T + jnp.arange(offsets.shape[0], dtype=jnp.int32)[None, :]]
    reshape x1, local copies, waits for them, and re-layouts: 0.76 us -> 0.08 us  [on_device_ring(): meta = jnp.concatenate([gauges, partners.reshape(-1)])]
    ppermute x5, starting transfers between devices: 0.71 us -> 1.21 us  [exchange(): return lax.ppermute(x, 'gy', [(0, 1), (1, 0)])]
  transfers between devices with their start and end apart: 15 -> 15, of which waited for: 9 -> 6; matrix products, arithmetic and copies ran while one was open for 6% -> 6% of each run, Pallas kernels for 2% -> 2%
where the time goes in v2:
time: 46.7 us; the launch traced here: 46.5 us
  waiting for transfers between devices  15.9 us (34%)
  Pallas kernels  14.3 us (31%)
  starting transfers between devices  12.6 us (27%)
  other arithmetic  3.31 us (7%)
    pallas_call x1, Pallas kernels, gram(): pl.pallas_call(functools.partial(gram_kernel, len(early) // 2, snaps, sca...  13.3 us
    ppermute x4, waiting for transfers between devices, onward(): b = lax.ppermute(b, 'gx', back)  9.7 us
    ppermute x4, starting transfers between devices, onward(): f = lax.ppermute(f, 'gx', ahead)  7.83 us
    ppermute x4, waiting for transfers between devices, onward(): f = lax.ppermute(f, 'gx', ahead)  5.92 us
    ppermute x2, starting transfers between devices, on_device_ring(): ef, eb = (lax.ppermute(extra, 'gx', ahead), lax.ppermute(extra, 'gx', back))  3.05 us
    ppermute x5, starting transfers between devices, exchange(): return lax.ppermute(x, 'gy', [(0, 1), (1, 0)])  1.21 us
    pallas_call x3, Pallas kernels, spectra_group(): pl.pallas_call(functools.partial(spectra_kernel, snaps), in_specs=[vmem]...  0.97 us
    concatenate x1, other arithmetic, on_device_ring(): own = jnp.concatenate([optical_phase, extra])  0.94 us
  transfers between devices with their start and end apart: 15, of which 6 were waited for; matrix products, arithmetic and copies ran while one was open for 6% of the time, Pallas kernels for 2%

profile of v2, /device:TPU:0, one launch (start us, length us, event | category | flops | bytes accessed | tf_op | source)
XLA Modules:
  0.0 46.5 jit_solution(12020947383212704023)
XLA Ops:
  0.0 0.7 %convert_element_type.40 = bf16[2]{0:T(256)(128)(2,1)S(1)} convert(s32[2]{0:T(128)} %param.6) | non-fusion elementwise | flops 2 | bytes 12 | tf_op jit(solution)/shard_map/convert_element_type | solution.py:239
  0.7 0.1 broadcast_in_dim.6
  0.7 0.1 broadcast_in_dim.7
  0.8 0.1 broadcast_in_dim.8
  0.9 3.0 %collective-permute-start.4 = (bf16[8,512]{1,0:T(8,128)(2,1)S(1)}, bf16[8,512]{1,0:T(8,128)(2,1)S(1)}, u32[]{:S(2)}, u32[]{:S(2)}) collective-permute-start(bf16[8,512]{1,0:T(8,128)(2,1)S(1)} %broadcast_in_dim.8), channel_id=1, source_target_pairs={{4,0},{8,4},{12,8},{14,12},{10,14},{6,10},{2,6},{0,2},{5,1},{9,5},... | collective-permute-start | bytes 24584 | tf_op jit(solution)/shard_map/ppermute | solution.py:242
  3.9 0.1 collective-permute-start.1
  4.0 2.0 %collective-permute-start = (bf16[192,512]{1,0:T(8,128)(2,1)}, bf16[192,512]{1,0:T(8,128)(2,1)S(1)}, u32[]{:S(2)}, u32[]{:S(2)}) collective-permute-start(bf16[192,512]{1,0:T(8,128)(2,1)} %param.4), channel_id=1, source_target_pairs={{0,4},{4,8},{8,12},{12,14},{14,10},{10,6},{6,2},{2,0},{1,5},{5,9},... | collective-permute-start | bytes 589832 | tf_op jit(solution)/shard_map/ppermute | solution.py:233
  6.0 0.0 collective-permute-start.3
  6.0 0.1 iota_add_fusion
  6.1 0.2 multiply_convert_fusion.2
  6.3 5.7 %collective-permute-done.3 = bf16[192,512]{1,0:T(8,128)(2,1)S(1)} collective-permute-done((bf16[192,512]{1,0:T(8,128)(2,1)}, bf16[192,512]{1,0:T(8,128)(2,1)S(1)}, u32[]{:S(2)}, u32[]{:S(2)}) %collective-permute-start.3) | collective-permute-done | bytes 196640 | tf_op jit(solution)/shard_map/ppermute | solution.py:234
  12.0 0.0 collective-permute-done.4
  12.0 0.4 collective-permute-start.6
  12.4 0.0 collective-permute-done
  12.4 0.0 collective-permute-done.1
  12.4 1.8 %collective-permute-start.2 = (bf16[200,512]{1,0:T(8,128)(2,1)S(1)}, bf16[200,512]{1,0:T(8,128)(2,1)S(1)}, u32[]{:S(2)}, u32[]{:S(2)}) collective-permute-start(bf16[200,512]{1,0:T(8,128)(2,1)S(1)} %constant_dynamic-update-slice_fusion.refs_1_), channel_id=1, source_target_pairs={{0,4},{4,8},{8,12},{12,14},{14,10},{10,6},{6,2},{2,0},{1,5},{5,9},... | collective-permute-start | bytes 614408 | tf_op jit(solution)/shard_map/ppermute | solution.py:233
  14.2 4.5 %collective-permute-done.2.refs_0_ = bf16[200,512]{1,0:T(8,128)(2,1)S(1)} collective-permute-done((bf16[200,512]{1,0:T(8,128)(2,1)S(1)}, bf16[200,512]{1,0:T(8,128)(2,1)S(1)}, u32[]{:S(2)}, u32[]{:S(2)}) %collective-permute-start.2) | collective-permute-done | bytes 204832 | tf_op jit(solution)/shard_map/ppermute | solution.py:233
  18.7 2.0 %collective-permute-start.8 = (bf16[200,512]{1,0:T(8,128)(2,1)S(1)}, bf16[200,512]{1,0:T(8,128)(2,1)S(1)}, u32[]{:S(2)}, u32[]{:S(2)}) collective-permute-start(bf16[200,512]{1,0:T(8,128)(2,1)S(1)} %collective-permute-done.2.refs_0_), channel_id=1, source_target_pairs={{0,4},{4,8},{8,12},{12,14},{14,10},{10,6},{6,2},{2,0},{1,5},{5,9},... | collective-permute-start | bytes 614408 | tf_op jit(solution)/shard_map/ppermute | solution.py:233
  20.7 0.0 collective-permute-done.6.refs_1_
  20.7 0.0 collective-permute-start.9
  20.7 0.9 %pad_maximum_fusion.refs_0_ = bf16[200,512]{1,0:T(8,128)(2,1)S(1)} fusion(bf16[8,512]{1,0:T(8,128)(2,1)S(1)} %broadcast_in_dim.8, bf16[192,512]{1,0:T(8,128)(2,1)} %param.4), kind=kLoop, calls=%fused_computation | loop fusion | flops 409600 | bytes 409600 | tf_op jit(solution)/shard_map/concatenate | solution.py:244
  21.6 0.4 spectra.3
  22.0 0.1 collective-permute-start.5
  22.1 0.3 spectra.4
  22.4 0.6 %collective-permute-start.7 = (f32[4,128,128]{2,1,0:T(8,128)S(1)}, f32[4,128,128]{2,1,0:T(8,128)S(1)}, u32[]{:S(2)}, u32[]{:S(2)}) collective-permute-start(f32[4,128,128]{2,1,0:T(8,128)S(1)} %get-tuple-element.20), channel_id=1, source_target_pairs={{0,1},{1,0},{2,3},{3,2},{4,5},{5,4},{6,7},{7,6},{8,9},{9,8},{10,11... | collective-permute-start | bytes 786440 | tf_op jit(solution)/shard_map/ppermute | solution.py:224
  23.0 4.0 %collective-permute-done.9.refs_1_ = bf16[200,512]{1,0:T(8,128)(2,1)S(1)} collective-permute-done((bf16[200,512]{1,0:T(8,128)(2,1)S(1)}, bf16[200,512]{1,0:T(8,128)(2,1)S(1)}, u32[]{:S(2)}, u32[]{:S(2)}) %collective-permute-start.9) | collective-permute-done | bytes 204832 | tf_op jit(solution)/shard_map/ppermute | solution.py:234
  26.9 0.1 collective-permute-start.12
  27.0 0.0 collective-permute-done.8.refs_0_
  27.0 2.1 %collective-permute-start.11 = (bf16[96,512]{1,0:T(8,128)(2,1)S(1)}, bf16[96,512]{1,0:T(8,128)(2,1)S(1)}, u32[]{:S(2)}, u32[]{:S(2)}) collective-permute-start(bf16[96,512]{1,0:T(8,128)(2,1)S(1)} %slice.8), channel_id=1, source_target_pairs={{0,4},{4,8},{8,12},{12,14},{14,10},{10,6},{6,2},{2,0},{1,5},{5,9},... | collective-permute-start | bytes 294920 | tf_op jit(solution)/shard_map/ppermute | solution.py:233
  29.1 0.3 spectra.5
  29.4 0.1 collective-permute-start.10
  29.5 0.7 %bitcast_add_fusion = s32[2,4]{1,0:T(2,128)S(1)} fusion(s32[4,2]{0,1:T(2,128)} %param.7), kind=kLoop, calls=%fused_computation.18 | loop fusion | flops 8 | bytes 64 | tf_op jit(solution)/shard_map/add | solution.py:248
  30.2 0.1 reshape.139
  30.3 1.5 %collective-permute-done.11.refs_6_ = bf16[96,512]{1,0:T(8,128)(2,1)S(1)} collective-permute-done((bf16[96,512]{1,0:T(8,128)(2,1)S(1)}, bf16[96,512]{1,0:T(8,128)(2,1)S(1)}, u32[]{:S(2)}, u32[]{:S(2)}) %collective-permute-start.11) | collective-permute-done | bytes 98336 | tf_op jit(solution)/shard_map/ppermute | solution.py:233
  31.7 0.0 collective-permute-start.13
  31.7 0.0 collective-permute-done.12.refs_7_
  31.7 0.5 %collective-permute-start.14 = (bf16[104,512]{1,0:T(8,128)(2,1)S(1)}, bf16[104,512]{1,0:T(8,128)(2,1)S(1)}, u32[]{:S(2)}, u32[]{:S(2)}) collective-permute-start(bf16[104,512]{1,0:T(8,128)(2,1)S(1)} %collective-permute-done.12.refs_7_), channel_id=1, source_target_pairs={{0,1},{1,0},{2,3},{3,2},{4,5},{5,4},{6,7},{7,6},{8,9},{9,8},{10,11... | collective-permute-start | bytes 319496 | tf_op jit(solution)/shard_map/ppermute | solution.py:224
  32.2 0.7 %pad_add_fusion.meta_ref = s32[12]{0:T(128)S(1)} fusion(s32[8]{0:T(128)S(1)} %reshape.139, s32[4]{0:T(128)} %param.5), kind=kLoop, calls=%fused_computation.20 | loop fusion | flops 12 | bytes 96 | tf_op jit(solution)/shard_map/concatenate | solution.py:249
  33.0 0.0 collective-permute-done.5.refs_1_
  33.0 0.0 collective-permute-done.7.refs_3_
  33.0 0.1 collective-permute-done.13.refs_8_
  33.0 0.2 collective-permute-done.14.refs_9_
  33.2 0.0 collective-permute-done.10.refs_5_
  33.2 13.3 %gram.1 = bf16[2,16,4,2,256,256]{5,4,3,2,1,0:T(8,128)(2,1)} custom-call(s32[12]{0:T(128)S(1)} %pad_add_fusion.meta_ref, f32[64,256]{1,0:T(8,128)S(1)} %pad_convert_fusion.base_ref, f32[4,192,128]{2,1,0:T(8,128)S(1)} %get-tuple-element.16.refs_0_, f32[4,192,128]{2,1,0:T(8,128)S(1)} %collective-permute-done.5.refs_1_, ...), custom_call_target="tpu_custom_call" | custom-call | tf_op jit(solution)/shard_map/gram/pallas_call | solution.py:182
  (10 shorter events, 0.1 us)
Async XLA Ops:
  0.9 11.1 %collective-permute-start.4 = (bf16[8,512]{1,0:T(8,128)(2,1)S(1)}, bf16[8,512]{1,0:T(8,128)(2,1)S(1)}, u32[]{:S(2)}, u32[]{:S(2)}) collective-permute-start(bf16[8,512]{1,0:T(8,128)(2,1)S(1)} %broadcast_in_dim.8), channel_id=1, source_target_pairs={{4,0},{8,4},{12,8},{14,12},{10,14},{6,10},{2,6},{0,2},{5,1},{9,5},... | collective-permute-start | bytes 24584 | tf_op jit(solution)/shard_map/ppermute | solution.py:242
  3.9 8.6 %collective-permute-start.1 = (bf16[8,512]{1,0:T(8,128)(2,1)S(1)}, bf16[8,512]{1,0:T(8,128)(2,1)S(1)}, u32[]{:S(2)}, u32[]{:S(2)}) collective-permute-start(bf16[8,512]{1,0:T(8,128)(2,1)S(1)} %broadcast_in_dim.8), channel_id=1, source_target_pairs={{0,4},{4,8},{8,12},{12,14},{14,10},{10,6},{6,2},{2,0},{1,5},{5,9},... | collective-permute-start | bytes 24584 | tf_op jit(solution)/shard_map/ppermute | solution.py:242
  4.0 8.4 %collective-permute-start = (bf16[192,512]{1,0:T(8,128)(2,1)}, bf16[192,512]{1,0:T(8,128)(2,1)S(1)}, u32[]{:S(2)}, u32[]{:S(2)}) collective-permute-start(bf16[192,512]{1,0:T(8,128)(2,1)} %param.4), channel_id=1, source_target_pairs={{0,4},{4,8},{8,12},{12,14},{14,10},{10,6},{6,2},{2,0},{1,5},{5,9},... | collective-permute-start | bytes 589832 | tf_op jit(solution)/shard_map/ppermute | solution.py:233
  6.0 6.0 %collective-permute-start.3 = (bf16[192,512]{1,0:T(8,128)(2,1)}, bf16[192,512]{1,0:T(8,128)(2,1)S(1)}, u32[]{:S(2)}, u32[]{:S(2)}) collective-permute-start(bf16[192,512]{1,0:T(8,128)(2,1)} %param.4), channel_id=1, source_target_pairs={{4,0},{8,4},{12,8},{14,12},{10,14},{6,10},{2,6},{0,2},{5,1},{9,5},... | collective-permute-start | bytes 589832 | tf_op jit(solution)/shard_map/ppermute | solution.py:234
  12.0 8.6 %collective-permute-start.6 = (bf16[200,512]{1,0:T(8,128)(2,1)S(1)}, bf16[200,512]{1,0:T(8,128)(2,1)S(1)}, u32[]{:S(2)}, u32[]{:S(2)}) collective-permute-start(bf16[200,512]{1,0:T(8,128)(2,1)S(1)} %constant_dynamic-update-slice_fusion.2.refs_2_), channel_id=1, source_target_pairs={{4,0},{8,4},{12,8},{14,12},{10,14},{6,10},{2,6},{0,2},{5,1},{9,5},... | collective-permute-start | bytes 614408 | tf_op jit(solution)/shard_map/ppermute | solution.py:234
  12.4 6.2 %collective-permute-start.2 = (bf16[200,512]{1,0:T(8,128)(2,1)S(1)}, bf16[200,512]{1,0:T(8,128)(2,1)S(1)}, u32[]{:S(2)}, u32[]{:S(2)}) collective-permute-start(bf16[200,512]{1,0:T(8,128)(2,1)S(1)} %constant_dynamic-update-slice_fusion.refs_1_), channel_id=1, source_target_pairs={{0,4},{4,8},{8,12},{12,14},{14,10},{10,6},{6,2},{2,0},{1,5},{5,9},... | collective-permute-start | bytes 614408 | tf_op jit(solution)/shard_map/ppermute | solution.py:233
  18.7 8.4 %collective-permute-start.8 = (bf16[200,512]{1,0:T(8,128)(2,1)S(1)}, bf16[200,512]{1,0:T(8,128)(2,1)S(1)}, u32[]{:S(2)}, u32[]{:S(2)}) collective-permute-start(bf16[200,512]{1,0:T(8,128)(2,1)S(1)} %collective-permute-done.2.refs_0_), channel_id=1, source_target_pairs={{0,4},{4,8},{8,12},{12,14},{14,10},{10,6},{6,2},{2,0},{1,5},{5,9},... | collective-permute-start | bytes 614408 | tf_op jit(solution)/shard_map/ppermute | solution.py:233
  20.7 6.3 %collective-permute-start.9 = (bf16[200,512]{1,0:T(8,128)(2,1)S(1)}, bf16[200,512]{1,0:T(8,128)(2,1)S(1)}, u32[]{:S(2)}, u32[]{:S(2)}) collective-permute-start(bf16[200,512]{1,0:T(8,128)(2,1)S(1)} %collective-permute-done.6.refs_1_), channel_id=1, source_target_pairs={{4,0},{8,4},{12,8},{14,12},{10,14},{6,10},{2,6},{0,2},{5,1},{9,5},... | collective-permute-start | bytes 614408 | tf_op jit(solution)/shard_map/ppermute | solution.py:234
  22.0 11.0 %collective-permute-start.5 = (f32[4,192,128]{2,1,0:T(8,128)S(1)}, f32[4,192,128]{2,1,0:T(8,128)S(1)}, u32[]{:S(2)}, u32[]{:S(2)}) collective-permute-start(f32[4,192,128]{2,1,0:T(8,128)S(1)} %get-tuple-element.17), channel_id=1, source_target_pairs={{0,1},{1,0},{2,3},{3,2},{4,5},{5,4},{6,7},{7,6},{8,9},{9,8},{10,11... | collective-permute-start | bytes 1179656 | tf_op jit(solution)/shard_map/ppermute | solution.py:224
  22.4 10.6 %collective-permute-start.7 = (f32[4,128,128]{2,1,0:T(8,128)S(1)}, f32[4,128,128]{2,1,0:T(8,128)S(1)}, u32[]{:S(2)}, u32[]{:S(2)}) collective-permute-start(f32[4,128,128]{2,1,0:T(8,128)S(1)} %get-tuple-element.20), channel_id=1, source_target_pairs={{0,1},{1,0},{2,3},{3,2},{4,5},{5,4},{6,7},{7,6},{8,9},{9,8},{10,11... | collective-permute-start | bytes 786440 | tf_op jit(solution)/shard_map/ppermute | solution.py:224
  26.9 4.8 %collective-permute-start.12 = (bf16[104,512]{1,0:T(8,128)(2,1)S(1)}, bf16[104,512]{1,0:T(8,128)(2,1)S(1)}, u32[]{:S(2)}, u32[]{:S(2)}) collective-permute-start(bf16[104,512]{1,0:T(8,128)(2,1)S(1)} %slice.9), channel_id=1, source_target_pairs={{4,0},{8,4},{12,8},{14,12},{10,14},{6,10},{2,6},{0,2},{5,1},{9,5},... | collective-permute-start | bytes 319496 | tf_op jit(solution)/shard_map/ppermute | solution.py:234
  27.0 4.7 %collective-permute-start.11 = (bf16[96,512]{1,0:T(8,128)(2,1)S(1)}, bf16[96,512]{1,0:T(8,128)(2,1)S(1)}, u32[]{:S(2)}, u32[]{:S(2)}) collective-permute-start(bf16[96,512]{1,0:T(8,128)(2,1)S(1)} %slice.8), channel_id=1, source_target_pairs={{0,4},{4,8},{8,12},{12,14},{14,10},{10,6},{6,2},{2,0},{1,5},{5,9},... | collective-permute-start | bytes 294920 | tf_op jit(solution)/shard_map/ppermute | solution.py:233
  29.4 3.8 %collective-permute-start.10 = (f32[4,128,128]{2,1,0:T(8,128)S(1)}, f32[4,128,128]{2,1,0:T(8,128)S(1)}, u32[]{:S(2)}, u32[]{:S(2)}) collective-permute-start(f32[4,128,128]{2,1,0:T(8,128)S(1)} %get-tuple-element.22), channel_id=1, source_target_pairs={{0,1},{1,0},{2,3},{3,2},{4,5},{5,4},{6,7},{7,6},{8,9},{9,8},{10,11... | collective-permute-start | bytes 786440 | tf_op jit(solution)/shard_map/ppermute | solution.py:224
  31.7 1.3 %collective-permute-start.13 = (bf16[96,512]{1,0:T(8,128)(2,1)S(1)}, bf16[96,512]{1,0:T(8,128)(2,1)S(1)}, u32[]{:S(2)}, u32[]{:S(2)}) collective-permute-start(bf16[96,512]{1,0:T(8,128)(2,1)S(1)} %collective-permute-done.11.refs_6_), channel_id=1, source_target_pairs={{0,1},{1,0},{2,3},{3,2},{4,5},{5,4},{6,7},{7,6},{8,9},{9,8},{10,11... | collective-permute-start | bytes 294920 | tf_op jit(solution)/shard_map/ppermute | solution.py:224
  31.7 1.5 %collective-permute-start.14 = (bf16[104,512]{1,0:T(8,128)(2,1)S(1)}, bf16[104,512]{1,0:T(8,128)(2,1)S(1)}, u32[]{:S(2)}, u32[]{:S(2)}) collective-permute-start(bf16[104,512]{1,0:T(8,128)(2,1)S(1)} %collective-permute-done.12.refs_7_), channel_id=1, source_target_pairs={{0,1},{1,0},{2,3},{3,2},{4,5},{5,4},{6,7},{7,6},{8,9},{9,8},{10,11... | collective-permute-start | bytes 319496 | tf_op jit(solution)/shard_map/ppermute | solution.py:224

commit v3 on v2

--- a/solution.py
+++ b/solution.py
@@ -108,7 +108,8 @@
 
     def copies(f, slot):
         return [
-            pltpu.make_async_copy(buf_ref.at[slot, part], out_ref.at[part, f], sems.at[slot, part])
+            pltpu.make_async_copy(buf_ref.at[slot, part, blk], out_ref.at[part, f, blk], sems.at[slot, part, blk])
+            for blk in range(blocks)
             for part in range(2)
         ]
 
@@ -144,8 +145,8 @@
                     tile = tile * scale
                 buf_ref[slot, 0, blk, k] = tile[:, :BLOCK].astype(jnp.bfloat16)
                 buf_ref[slot, 1, blk, k] = tile[:, BLOCK:].astype(jnp.bfloat16)
-        for c in copies(f, slot):
-            c.start()
+            for c in copies(f, slot)[2 * blk : 2 * blk + 2]:
+                c.start()
 
     def free(f):
         @pl.when(f >= slots)
@@ -188,7 +189,7 @@
             pltpu.VMEM((2 * half, total, LANES), jnp.float32),
             *[pltpu.VMEM((blocks, 2 * count * snaps, 2 * BLOCK), jnp.bfloat16)] * 4,
             pltpu.VMEM((slots, 2, blocks, PARTNERS, BLOCK, BLOCK), jnp.bfloat16),
-            pltpu.SemaphoreType.DMA((slots, 2)),
+            pltpu.SemaphoreType.DMA((slots, 2, blocks)),
         ],
         compiler_params=pltpu.CompilerParams(vmem_limit_bytes=24 << 20),
         name="gram",
@@ -202,8 +203,6 @@
     bins_dev = BINS // (count * pair_devices)
     snaps = snap_starts.shape[0]
     order = ring_order(count)
-    ahead = [(order[i], order[(i + 1) % count]) for i in range(count)]
-    back = [(b, a) for a, b in ahead]
 
     scale = 1.0 / math.sqrt(count * snaps)
     root = math.sqrt(scale)
@@ -229,9 +228,12 @@
     def spectra(*stretches):
         return spectra_group(snaps, base, stretches)
 
-    def onward(f, b):
-        f = lax.ppermute(f, "gx", ahead)
-        b = lax.ppermute(b, "gx", back)
+    def moved(x, places):
+        return lax.ppermute(x, "gx", [(order[i], order[(i + places) % count]) for i in range(count)])
+
+    def onward(f, b, places=1):
+        f = moved(f, places)
+        b = moved(b, -places)
         return f, b
 
     half_rows = rows_local // 2
@@ -239,19 +241,20 @@
     extra = snap_starts.astype(optical_phase.dtype)[:, None, None]
     extra = jnp.broadcast_to(extra, (snaps, 8 // snaps, half)).reshape(8, half)
     f1, b1 = onward(optical_phase, optical_phase)
-    ef, eb = lax.ppermute(extra, "gx", ahead), lax.ppermute(extra, "gx", back)
+    ef, eb = onward(extra, extra)
     f1, b1 = jnp.concatenate([f1, ef]), jnp.concatenate([b1, eb])
     own = jnp.concatenate([optical_phase, extra])
     f2, b2 = onward(f1, b1)
     near1, far1 = spectra(own, f1, b1)
-    f2, gauges, offsets = tie(f2, gauge_length, partner_offsets)
+    near1, gauges, offsets = tie(near1, gauge_length, partner_offsets)
     partners = offsets.T + jnp.arange(offsets.shape[0], dtype=jnp.int32)[None, :]
     meta = jnp.concatenate([gauges, partners.reshape(-1)])
+    other1 = exchange(far1)
     f3, b3 = onward(f2, b2)
-    other1 = exchange(far1)
+    f4, b4 = onward(f2[:half_rows], b2[half_rows:], 2)
     near2, far2 = spectra(f2, b2)
-    f4, b4 = onward(f3[:half_rows], b3[half_rows:])
     other2 = exchange(far2)
+    b4, meta = tie(b4, meta)
     near3, far3 = spectra(f3, b3)
     s_b4 = exchange(b4)
     s_f4 = exchange(f4)

time: 46.7 us -> 51.6 us (1.10)
  waiting for transfers between devices: 15.9 us -> 19.9 us
  starting transfers between devices: 12.6 us -> 13.5 us
    ppermute x10, waiting for transfers between devices: 15.6 us -> 19 us  [moved(): lax.ppermute(x, 'gx', [(order[i], order[(i + places) % count]) for i in r...]
    ppermute x10, starting transfers between devices: 11.3 us -> 12.3 us  [moved(): lax.ppermute(x, 'gx', [(order[i], order[(i + places) % count]) for i in r...]
    ppermute x5, waiting for transfers between devices: 0.23 us -> 0.95 us  [exchange(): return lax.ppermute(x, 'gy', [(0, 1), (1, 0)])]
  transfers between devices with their start and end apart: 15 -> 15, of which waited for: 6 -> 7; matrix products, arithmetic and copies ran while one was open for 6% -> 5% of each run, Pallas kernels for 2% -> 2%
where the time goes in v3:
time: 51.6 us; the launch traced here: 51.4 us
  waiting for transfers between devices  19.9 us (39%)
  Pallas kernels  14.1 us (27%)
  starting transfers between devices  13.5 us (26%)
  other arithmetic  3.31 us (6%)
    ppermute x10, waiting for transfers between devices, moved(): lax.ppermute(x, 'gx', [(order[i], order[(i + places) % count]) for i in r...  19 us
    pallas_call x1, Pallas kernels, gram(): pl.pallas_call(functools.partial(gram_kernel, len(early) // 2, snaps, sca...  13.2 us
    ppermute x10, starting transfers between devices, moved(): lax.ppermute(x, 'gx', [(order[i], order[(i + places) % count]) for i in r...  12.3 us
    ppermute x5, starting transfers between devices, exchange(): return lax.ppermute(x, 'gy', [(0, 1), (1, 0)])  1.21 us
  transfers between devices with their start and end apart: 15, of which 7 were waited for; matrix products, arithmetic and copies ran while one was open for 5% of the time, Pallas kernels for 2%

profile of v3, /device:TPU:0, one launch (start us, length us, event | category | flops | bytes accessed | tf_op | source)
XLA Modules:
  0.0 51.4 jit_solution(6417611222254517206)
XLA Ops:
  0.0 0.7 %convert_element_type.40 = bf16[2]{0:T(256)(128)(2,1)S(1)} convert(s32[2]{0:T(128)} %param.6) | non-fusion elementwise | flops 2 | bytes 12 | tf_op jit(solution)/shard_map/convert_element_type | solution.py:241
  0.7 0.1 broadcast_in_dim.6
  0.7 0.1 broadcast_in_dim.7
  0.8 0.1 broadcast_in_dim.8
  0.9 3.1 %collective-permute-start.5 = (bf16[8,512]{1,0:T(8,128)(2,1)S(1)}, bf16[8,512]{1,0:T(8,128)(2,1)S(1)}, u32[]{:S(2)}, u32[]{:S(2)}) collective-permute-start(bf16[8,512]{1,0:T(8,128)(2,1)S(1)} %broadcast_in_dim.8), channel_id=1, source_target_pairs={{0,4},{4,8},{8,12},{12,14},{14,10},{10,6},{6,2},{2,0},{1,5},{5,9},... | collective-permute-start | bytes 24584 | tf_op jit(solution)/shard_map/ppermute | solution.py:232
  3.9 0.0 collective-permute-start.1
  4.0 1.9 %collective-permute-start = (bf16[192,512]{1,0:T(8,128)(2,1)}, bf16[192,512]{1,0:T(8,128)(2,1)S(1)}, u32[]{:S(2)}, u32[]{:S(2)}) collective-permute-start(bf16[192,512]{1,0:T(8,128)(2,1)} %param.4), channel_id=1, source_target_pairs={{0,2},{4,0},{8,4},{12,8},{14,12},{10,14},{6,10},{2,6},{1,3},{5,1},... | collective-permute-start | bytes 589832 | tf_op jit(solution)/shard_map/ppermute | solution.py:232
  5.9 0.1 collective-permute-start.4
  6.1 0.1 iota_add_fusion
  6.1 0.2 multiply_convert_fusion.2
  6.3 5.6 %collective-permute-done.4 = bf16[192,512]{1,0:T(8,128)(2,1)S(1)} collective-permute-done((bf16[192,512]{1,0:T(8,128)(2,1)}, bf16[192,512]{1,0:T(8,128)(2,1)S(1)}, u32[]{:S(2)}, u32[]{:S(2)}) %collective-permute-start.4) | collective-permute-done | bytes 196640 | tf_op jit(solution)/shard_map/ppermute | solution.py:232
  11.9 0.0 collective-permute-done.5
  11.9 0.4 collective-permute-start.7
  12.4 0.0 collective-permute-done
  12.4 0.0 collective-permute-done.1
  12.4 1.7 %collective-permute-start.2 = (bf16[200,512]{1,0:T(8,128)(2,1)S(1)}, bf16[200,512]{1,0:T(8,128)(2,1)S(1)}, u32[]{:S(2)}, u32[]{:S(2)}) collective-permute-start(bf16[200,512]{1,0:T(8,128)(2,1)S(1)} %constant_dynamic-update-slice_fusion.refs_2_), channel_id=1, source_target_pairs={{0,2},{4,0},{8,4},{12,8},{14,12},{10,14},{6,10},{2,6},{1,3},{5,1},... | collective-permute-start | bytes 614408 | tf_op jit(solution)/shard_map/ppermute | solution.py:232
  14.1 4.0 %collective-permute-done.7.refs_0_ = bf16[200,512]{1,0:T(8,128)(2,1)S(1)} collective-permute-done((bf16[200,512]{1,0:T(8,128)(2,1)S(1)}, bf16[200,512]{1,0:T(8,128)(2,1)S(1)}, u32[]{:S(2)}, u32[]{:S(2)}) %collective-permute-start.7) | collective-permute-done | bytes 204832 | tf_op jit(solution)/shard_map/ppermute | solution.py:232
  18.2 0.1 collective-permute-start.9
  18.3 0.4 collective-permute-done.2.refs_1_
  18.6 1.9 %collective-permute-start.10 = (bf16[200,512]{1,0:T(8,128)(2,1)S(1)}, bf16[200,512]{1,0:T(8,128)(2,1)S(1)}, u32[]{:S(2)}, u32[]{:S(2)}) collective-permute-start(bf16[200,512]{1,0:T(8,128)(2,1)S(1)} %collective-permute-done.2.refs_1_), channel_id=1, source_target_pairs={{0,2},{4,0},{8,4},{12,8},{14,12},{10,14},{6,10},{2,6},{1,3},{5,1},... | collective-permute-start | bytes 614408 | tf_op jit(solution)/shard_map/ppermute | solution.py:232
  20.6 0.9 %pad_maximum_fusion.refs_0_ = bf16[200,512]{1,0:T(8,128)(2,1)S(1)} fusion(bf16[8,512]{1,0:T(8,128)(2,1)S(1)} %broadcast_in_dim.8, bf16[192,512]{1,0:T(8,128)(2,1)} %param.4), kind=kLoop, calls=%fused_computation | loop fusion | flops 409600 | bytes 409600 | tf_op jit(solution)/shard_map/concatenate | solution.py:246
  21.5 0.3 spectra.3
  21.9 0.1 collective-permute-start.6
  22.0 0.3 spectra.4
  22.3 0.6 %collective-permute-start.8 = (f32[4,128,128]{2,1,0:T(8,128)S(1)}, f32[4,128,128]{2,1,0:T(8,128)S(1)}, u32[]{:S(2)}, u32[]{:S(2)}) collective-permute-start(f32[4,128,128]{2,1,0:T(8,128)S(1)} %get-tuple-element.23), channel_id=1, source_target_pairs={{0,1},{1,0},{2,3},{3,2},{4,5},{5,4},{6,7},{7,6},{8,9},{9,8},{10,11... | collective-permute-start | bytes 786440 | tf_op jit(solution)/shard_map/ppermute | solution.py:223
  22.8 1.1 %collective-permute-done.9.refs_0_ = bf16[200,512]{1,0:T(8,128)(2,1)S(1)} collective-permute-done((bf16[200,512]{1,0:T(8,128)(2,1)S(1)}, bf16[200,512]{1,0:T(8,128)(2,1)S(1)}, u32[]{:S(2)}, u32[]{:S(2)}) %collective-permute-start.9) | collective-permute-done | bytes 204832 | tf_op jit(solution)/shard_map/ppermute | solution.py:232
  23.9 0.5 collective-permute-done.10.refs_1_
  24.4 0.3 spectra.5
  24.7 0.1 collective-permute-start.11
  24.8 0.7 %bitcast_add_fusion = s32[2,4]{1,0:T(2,128)S(1)} fusion(s32[4,2]{0,1:T(2,128)} %param.7), kind=kLoop, calls=%fused_computation.18 | loop fusion | flops 8 | bytes 64 | tf_op jit(solution)/shard_map/add | solution.py:250
  25.5 0.1 reshape.140
  25.6 2.8 %collective-permute-start.12 = (bf16[96,512]{1,0:T(8,128)(2,1)S(1)}, bf16[96,512]{1,0:T(8,128)(2,1)S(1)}, u32[]{:S(2)}, u32[]{:S(2)}) collective-permute-start(bf16[96,512]{1,0:T(8,128)(2,1)S(1)} %slice.9), channel_id=1, source_target_pairs={{0,8},{4,12},{8,14},{12,10},{14,6},{10,2},{6,0},{2,4},{1,9},{5,13}... | collective-permute-start | bytes 294920 | tf_op jit(solution)/shard_map/ppermute | solution.py:232
  28.4 0.3 collective-permute-start.3
  28.6 0.7 %pad_add_fusion.meta_ref = s32[12]{0:T(128)S(1)} fusion(s32[8]{0:T(128)S(1)} %reshape.140, s32[4]{0:T(128)} %param.5), kind=kLoop, calls=%fused_computation.20 | loop fusion | flops 12 | bytes 96 | tf_op jit(solution)/shard_map/concatenate | solution.py:251
  29.4 7.4 %collective-permute-done.3.refs_7_ = bf16[104,512]{1,0:T(8,128)(2,1)S(1)} collective-permute-done((bf16[104,512]{1,0:T(8,128)(2,1)S(1)}, bf16[104,512]{1,0:T(8,128)(2,1)S(1)}, u32[]{:S(2)}, u32[]{:S(2)}) %collective-permute-start.3) | collective-permute-done | bytes 106528 | tf_op jit(solution)/shard_map/ppermute | solution.py:232
  36.7 0.0 collective-permute-start.14
  36.7 0.0 collective-permute-done.12.refs_6_
  36.7 0.5 collective-permute-start.13
  37.3 0.0 collective-permute-done.6.refs_1_
  37.3 0.9 %collective-permute-done.13.refs_8_ = bf16[96,512]{1,0:T(8,128)(2,1)S(1)} collective-permute-done((bf16[96,512]{1,0:T(8,128)(2,1)S(1)}, bf16[96,512]{1,0:T(8,128)(2,1)S(1)}, u32[]{:S(2)}, u32[]{:S(2)}) %collective-permute-start.13) | collective-permute-done | bytes 98336 | tf_op jit(solution)/shard_map/ppermute | solution.py:223
  38.2 0.0 collective-permute-done.14.refs_9_
  38.2 0.0 collective-permute-done.8.refs_3_
  38.2 0.0 collective-permute-done.11.refs_5_
  38.2 13.2 %gram.1 = bf16[2,16,4,2,256,256]{5,4,3,2,1,0:T(8,128)(2,1)} custom-call(s32[12]{0:T(128)S(1)} %pad_add_fusion.meta_ref, f32[64,256]{1,0:T(8,128)S(1)} %pad_convert_fusion.base_ref, f32[4,192,128]{2,1,0:T(8,128)S(1)} %get-tuple-element.20.refs_0_, f32[4,192,128]{2,1,0:T(8,128)S(1)} %collective-permute-done.6.refs_1_, ...), custom_call_target="tpu_custom_call" | custom-call | tf_op jit(solution)/shard_map/gram/pallas_call | solution.py:183
  (10 shorter events, 0.1 us)
Async XLA Ops:
  0.9 11.0 %collective-permute-start.5 = (bf16[8,512]{1,0:T(8,128)(2,1)S(1)}, bf16[8,512]{1,0:T(8,128)(2,1)S(1)}, u32[]{:S(2)}, u32[]{:S(2)}) collective-permute-start(bf16[8,512]{1,0:T(8,128)(2,1)S(1)} %broadcast_in_dim.8), channel_id=1, source_target_pairs={{0,4},{4,8},{8,12},{12,14},{14,10},{10,6},{6,2},{2,0},{1,5},{5,9},... | collective-permute-start | bytes 24584 | tf_op jit(solution)/shard_map/ppermute | solution.py:232
  3.9 8.5 %collective-permute-start.1 = (bf16[8,512]{1,0:T(8,128)(2,1)S(1)}, bf16[8,512]{1,0:T(8,128)(2,1)S(1)}, u32[]{:S(2)}, u32[]{:S(2)}) collective-permute-start(bf16[8,512]{1,0:T(8,128)(2,1)S(1)} %broadcast_in_dim.8), channel_id=1, source_target_pairs={{0,2},{4,0},{8,4},{12,8},{14,12},{10,14},{6,10},{2,6},{1,3},{5,1},... | collective-permute-start | bytes 24584 | tf_op jit(solution)/shard_map/ppermute | solution.py:232
  4.0 8.4 %collective-permute-start = (bf16[192,512]{1,0:T(8,128)(2,1)}, bf16[192,512]{1,0:T(8,128)(2,1)S(1)}, u32[]{:S(2)}, u32[]{:S(2)}) collective-permute-start(bf16[192,512]{1,0:T(8,128)(2,1)} %param.4), channel_id=1, source_target_pairs={{0,2},{4,0},{8,4},{12,8},{14,12},{10,14},{6,10},{2,6},{1,3},{5,1},... | collective-permute-start | bytes 589832 | tf_op jit(solution)/shard_map/ppermute | solution.py:232
  5.9 6.0 %collective-permute-start.4 = (bf16[192,512]{1,0:T(8,128)(2,1)}, bf16[192,512]{1,0:T(8,128)(2,1)S(1)}, u32[]{:S(2)}, u32[]{:S(2)}) collective-permute-start(bf16[192,512]{1,0:T(8,128)(2,1)} %param.4), channel_id=1, source_target_pairs={{0,4},{4,8},{8,12},{12,14},{14,10},{10,6},{6,2},{2,0},{1,5},{5,9},... | collective-permute-start | bytes 589832 | tf_op jit(solution)/shard_map/ppermute | solution.py:232
  11.9 6.2 %collective-permute-start.7 = (bf16[200,512]{1,0:T(8,128)(2,1)S(1)}, bf16[200,512]{1,0:T(8,128)(2,1)S(1)}, u32[]{:S(2)}, u32[]{:S(2)}) collective-permute-start(bf16[200,512]{1,0:T(8,128)(2,1)S(1)} %constant_dynamic-update-slice_fusion.2.refs_1_), channel_id=1, source_target_pairs={{0,4},{4,8},{8,12},{12,14},{14,10},{10,6},{6,2},{2,0},{1,5},{5,9},... | collective-permute-start | bytes 614408 | tf_op jit(solution)/shard_map/ppermute | solution.py:232
  12.4 6.2 %collective-permute-start.2 = (bf16[200,512]{1,0:T(8,128)(2,1)S(1)}, bf16[200,512]{1,0:T(8,128)(2,1)S(1)}, u32[]{:S(2)}, u32[]{:S(2)}) collective-permute-start(bf16[200,512]{1,0:T(8,128)(2,1)S(1)} %constant_dynamic-update-slice_fusion.refs_2_), channel_id=1, source_target_pairs={{0,2},{4,0},{8,4},{12,8},{14,12},{10,14},{6,10},{2,6},{1,3},{5,1},... | collective-permute-start | bytes 614408 | tf_op jit(solution)/shard_map/ppermute | solution.py:232
  18.2 5.8 %collective-permute-start.9 = (bf16[200,512]{1,0:T(8,128)(2,1)S(1)}, bf16[200,512]{1,0:T(8,128)(2,1)S(1)}, u32[]{:S(2)}, u32[]{:S(2)}) collective-permute-start(bf16[200,512]{1,0:T(8,128)(2,1)S(1)} %collective-permute-done.7.refs_0_), channel_id=1, source_target_pairs={{0,4},{4,8},{8,12},{12,14},{14,10},{10,6},{6,2},{2,0},{1,5},{5,9},... | collective-permute-start | bytes 614408 | tf_op jit(solution)/shard_map/ppermute | solution.py:232
  18.6 5.8 %collective-permute-start.10 = (bf16[200,512]{1,0:T(8,128)(2,1)S(1)}, bf16[200,512]{1,0:T(8,128)(2,1)S(1)}, u32[]{:S(2)}, u32[]{:S(2)}) collective-permute-start(bf16[200,512]{1,0:T(8,128)(2,1)S(1)} %collective-permute-done.2.refs_1_), channel_id=1, source_target_pairs={{0,2},{4,0},{8,4},{12,8},{14,12},{10,14},{6,10},{2,6},{1,3},{5,1},... | collective-permute-start | bytes 614408 | tf_op jit(solution)/shard_map/ppermute | solution.py:232
  21.9 15.4 %collective-permute-start.6 = (f32[4,192,128]{2,1,0:T(8,128)S(1)}, f32[4,192,128]{2,1,0:T(8,128)S(1)}, u32[]{:S(2)}, u32[]{:S(2)}) collective-permute-start(f32[4,192,128]{2,1,0:T(8,128)S(1)} %get-tuple-element.21), channel_id=1, source_target_pairs={{0,1},{1,0},{2,3},{3,2},{4,5},{5,4},{6,7},{7,6},{8,9},{9,8},{10,11... | collective-permute-start | bytes 1179656 | tf_op jit(solution)/shard_map/ppermute | solution.py:223
  22.3 15.9 %collective-permute-start.8 = (f32[4,128,128]{2,1,0:T(8,128)S(1)}, f32[4,128,128]{2,1,0:T(8,128)S(1)}, u32[]{:S(2)}, u32[]{:S(2)}) collective-permute-start(f32[4,128,128]{2,1,0:T(8,128)S(1)} %get-tuple-element.23), channel_id=1, source_target_pairs={{0,1},{1,0},{2,3},{3,2},{4,5},{5,4},{6,7},{7,6},{8,9},{9,8},{10,11... | collective-permute-start | bytes 786440 | tf_op jit(solution)/shard_map/ppermute | solution.py:223
  24.7 13.5 %collective-permute-start.11 = (f32[4,128,128]{2,1,0:T(8,128)S(1)}, f32[4,128,128]{2,1,0:T(8,128)S(1)}, u32[]{:S(2)}, u32[]{:S(2)}) collective-permute-start(f32[4,128,128]{2,1,0:T(8,128)S(1)} %get-tuple-element.25), channel_id=1, source_target_pairs={{0,1},{1,0},{2,3},{3,2},{4,5},{5,4},{6,7},{7,6},{8,9},{9,8},{10,11... | collective-permute-start | bytes 786440 | tf_op jit(solution)/shard_map/ppermute | solution.py:223
  25.6 11.2 %collective-permute-start.12 = (bf16[96,512]{1,0:T(8,128)(2,1)S(1)}, bf16[96,512]{1,0:T(8,128)(2,1)S(1)}, u32[]{:S(2)}, u32[]{:S(2)}) collective-permute-start(bf16[96,512]{1,0:T(8,128)(2,1)S(1)} %slice.9), channel_id=1, source_target_pairs={{0,8},{4,12},{8,14},{12,10},{14,6},{10,2},{6,0},{2,4},{1,9},{5,13}... | collective-permute-start | bytes 294920 | tf_op jit(solution)/shard_map/ppermute | solution.py:232
  28.4 8.4 %collective-permute-start.3 = (bf16[104,512]{1,0:T(8,128)(2,1)S(1)}, bf16[104,512]{1,0:T(8,128)(2,1)S(1)}, u32[]{:S(2)}, u32[]{:S(2)}) collective-permute-start(bf16[104,512]{1,0:T(8,128)(2,1)S(1)} %slice.8), channel_id=1, source_target_pairs={{0,6},{4,2},{8,0},{12,4},{14,8},{10,12},{6,14},{2,10},{1,7},{5,3},... | collective-permute-start | bytes 319496 | tf_op jit(solution)/shard_map/ppermute | solution.py:232
  36.7 1.5 %collective-permute-start.14 = (bf16[104,512]{1,0:T(8,128)(2,1)S(1)}, bf16[104,512]{1,0:T(8,128)(2,1)S(1)}, u32[]{:S(2)}, u32[]{:S(2)}) collective-permute-start(bf16[104,512]{1,0:T(8,128)(2,1)S(1)} %collective-permute-done.3.refs_7_), channel_id=1, source_target_pairs={{0,1},{1,0},{2,3},{3,2},{4,5},{5,4},{6,7},{7,6},{8,9},{9,8},{10,11... | collective-permute-start | bytes 319496 | tf_op jit(solution)/shard_map/ppermute | solution.py:223
  36.7 1.5 %collective-permute-start.13 = (bf16[96,512]{1,0:T(8,128)(2,1)S(1)}, bf16[96,512]{1,0:T(8,128)(2,1)S(1)}, u32[]{:S(2)}, u32[]{:S(2)}) collective-permute-start(bf16[96,512]{1,0:T(8,128)(2,1)S(1)} %collective-permute-done.12.refs_6_), channel_id=1, source_target_pairs={{0,1},{1,0},{2,3},{3,2},{4,5},{5,4},{6,7},{7,6},{8,9},{9,8},{10,11... | collective-permute-start | bytes 294920 | tf_op jit(solution)/shard_map/ppermute | solution.py:223
